TPU v7x, 256 devices: a whole 4x4x8 slice. The times are simulated.
256 devices in a mesh: gz: 4 (over x), dev: 64 (over z, y, core).
Axes of the slice: x: 4, y: 4, z: 8, core: 2. Of those that a mesh axis runs over, the one named last changes fastest.
Arguments:
- source: float32 [512, 8, 16384], P(None, None, ('gz', 'dev')), may hold values from -6 to 6
- interior_inverse: float32 [512, 512], replicated, as said below
- coupling: float32 [512, 384], replicated, may hold values from -0.25 to 0.25
- trace_operator: float32 [384, 384], replicated, as said below
- face_ids: int32 [16384, 4], P(('gz', 'dev')), may hold values from 0 to 8191, as said below
- orientation: int32 [16384, 6], P(('gz', 'dev')), may hold values from 0 to 7
- element_scale: int32 [16384], P(('gz', 'dev')), may hold values from 1 to 4
Outputs:
- interior: float32 [512, 8, 16384], P(None, None, ('gz', 'dev'))
- side_traces: float32 [64, 8, 32768], P(None, None, ('gz', 'dev'))
- top_traces: float32 [64, 8, 16384], P(None, None, ('gz', 'dev'))
Inputs may be any that keep to these rules, and one draw needn't show every extreme that they name: `face_ids`: elements come in blocks of 64 (block b of a layer is the layer's elements b * 64 onward) and a layer's side faces in blocks of 128; face f of a layer belongs to block f // 128. Columns 0 and 1 of a block's elements name each face of that block exactly once. Columns 2 and 3 of a layer's elements name each face of the layer exactly once. The elements of one block name, in columns 2 and 3, at most 1 faces of any one other block, and in every layer some block reaches 1 with some other block. `interior_inverse`: symmetric positive definite. `trace_operator`: symmetric positive definite.
All inputs are finite; a program needn't handle non-finite values.
Results may differ from a plain program's by a relative error of at most 0.0001.
Values sent between devices are 32-bit elements; how exact they have to be, the bound alone decides.
A program may use at most 64 MiB of HBM per device.

v0:
```python
import functools

import jax
import jax.numpy as jnp
from jax import lax
from jax.experimental import pallas as pl
from jax.experimental.pallas import tpu as pltpu
from jax.sharding import PartitionSpec as P

MESH = pl.DeviceIdType.MESH
F32 = jnp.float32
BF16 = jnp.bfloat16
LANES = 128
ELEMENTS = 64
RIGHT = 8
NODES = 512
LOCAL = 384
ROWS = RIGHT * ELEMENTS
PAIRS = RIGHT // 2


def partner(me, turn, count):
    if count != 64:
        return (me + 1 + turn) % count
    far_z, far_y, far_core = turn // 8, turn % 8 // 2, turn % 2
    step_z = (4 + (far_z + 1) // 2 * (1 - 2 * (far_z % 2))) % 8
    step_y = (2 + (far_y + 1) // 2 * (1 - 2 * (far_y % 2))) % 4
    z = (me // 8 + step_z) % 8
    y = (me % 8 // 2 + step_y) % 4
    core = (me % 2 + 1 - far_core) % 2
    return z * 8 + y * 2 + core


def halves(value):
    high = value.astype(BF16)
    return high, (value - high.astype(F32)).astype(BF16)


def dot(left, right):
    return jnp.dot(left, right, preferred_element_type=F32)


def dot_three(left_high, left_low, right_high, right_low):
    return dot(left_high, right_high) + (dot(left_high, right_low) + dot(left_low, right_high))


def pick(onehot, value):
    high, low = halves(value)
    return dot(onehot, high) + dot(onehot, low)


def lane_of(shape):
    return lax.broadcasted_iota(jnp.int32, shape, 1)


def row_of(shape):
    return lax.broadcasted_iota(jnp.int32, shape, 0)


def swap_pair(first, second):
    low = lane_of(first.shape) < 64
    return (
        jnp.where(low, first, pltpu.roll(second, 64, 1)),
        jnp.where(low, pltpu.roll(first, 64, 1), second),
    )


def turned(value, index):
    return jnp.take_along_axis(value, index, axis=1, mode="promise_in_bounds")


def kernel(
    layers,
    blocks,
    source_hbm,
    inverse_hbm,
    coupling_hbm,
    operator_hbm,
    faces_ref,
    codes_ref,
    scale_ref,
    interior_hbm,
    sides_hbm,
    tops_hbm,
    source,
    inverse,
    coupling,
    operator,
    source_h,
    source_l,
    inverse_h,
    inverse_l,
    coupling_h,
    coupling_l,
    operator_h,
    operator_l,
    merged_h,
    merged_l,
    merged_th,
    merged_tl,
    table,
    index_to,
    index_from,
    scales,
    first,
    image,
    update,
    vector_h,
    vector_l,
    slots_first,
    slots_second,
    bottoms,
    tops,
    solved,
    moved_zero,
    moved_one,
    sides_zero,
    sides_one,
    tops_zero,
    tops_one,
    named_out,
    named_in,
    sent,
    received,
    got_bottoms,
    got_tops,
    sum_out,
    sum_in,
    layer_out,
    layer_in,
    load_sem,
    store_sem,
    named_sem,
    swap_sem,
    up_sem,
    down_sem,
    sum_sem,
    layer_sem,
):
    layer = lax.axis_index("gz")
    me = lax.axis_index("dev")
    others = blocks - 1

    barrier = pltpu.get_barrier_semaphore()

    def greet(turn, carry):
        pl.semaphore_signal(
            barrier, inc=1, device_id={"dev": partner(me, turn, blocks)}, device_id_type=MESH
        )
        return carry

    lax.fori_loop(0, others, greet, 0)
    for step in range(1, layers):
        pl.semaphore_signal(
            barrier, inc=1, device_id={"gz": (layer + step) % layers}, device_id_type=MESH
        )

    loads = [
        pltpu.make_async_copy(inverse_hbm, inverse, load_sem.at[0]),
        pltpu.make_async_copy(coupling_hbm, coupling, load_sem.at[1]),
        pltpu.make_async_copy(source_hbm, source, load_sem.at[2]),
        pltpu.make_async_copy(operator_hbm, operator, load_sem.at[3]),
    ]
    for load in loads:
        load.start()

    here = pl.ds(pl.multiple_of(me * 8, 8), 8)
    for phase in range(2):
        received[phase, here, :] = jnp.zeros((8, LANES), F32)
    named_in[me] = jnp.zeros((1, LANES), F32)

    @pl.when(layer == 0)
    def _():
        got_bottoms[...] = jnp.zeros(got_bottoms.shape, F32)

    @pl.when(layer == layers - 1)
    def _():
        got_tops[...] = jnp.zeros(got_tops.shape, F32)

    table[...] = jnp.zeros(table.shape, F32)
    faces = faces_ref[...].astype(F32)
    codes = codes_ref[...].astype(F32)
    for row in range(2):
        table[row : row + 1, 0:64] = faces[2 * row : 2 * row + 1]
        table[row : row + 1, 64:128] = faces[2 * row + 1 : 2 * row + 2]
    for row in range(3):
        table[2 + row : 3 + row, 0:64] = codes[2 * row : 2 * row + 1]
        table[2 + row : 3 + row, 64:128] = codes[2 * row + 1 : 2 * row + 2]
    table[5:6, 0:64] = scale_ref[...].astype(F32)
    columns = jnp.transpose(table[...])
    square = (LANES, LANES)
    first_row = jnp.broadcast_to(table[0:1, :], square).astype(jnp.int32) - me * LANES
    second_row = jnp.broadcast_to(table[1:2, :], square).astype(jnp.int32)
    first_col = jnp.broadcast_to(columns[:, 0:1], square).astype(jnp.int32) - me * LANES
    second_col = jnp.broadcast_to(columns[:, 1:2], square).astype(jnp.int32)

    def onehot(condition):
        return jnp.where(condition, 1.0, 0.0).astype(F32)

    near = onehot(first_col + me * LANES == second_row).astype(BF16)
    near_back = onehot(first_row + me * LANES == second_col).astype(BF16)
    into_faces = onehot(first_row == row_of(square)).astype(BF16)
    peers = (blocks, LANES)
    owner_row = second_row[:blocks] // LANES
    peer_row = row_of(peers)
    to_owner_f = onehot((owner_row == peer_row) & (peer_row != me))
    to_owner = to_owner_f.astype(BF16)
    from_owner = jnp.transpose(to_owner_f).astype(BF16)
    slot_number = (second_row[:blocks] % LANES + 1).astype(F32)
    named = jnp.sum(to_owner_f * slot_number, axis=1, keepdims=True)
    named = jnp.broadcast_to(named, peers)
    for peer in range(blocks):
        named_out[peer] = named[peer : peer + 1, :]

    lane = lane_of((ELEMENTS, LANES))
    low = lane < 64
    node_a, node_b = lane % 64 // 8, lane % 8
    for chunk in range(3):
        code = jnp.where(
            low,
            jnp.broadcast_to(columns[0:64, 2 + chunk : 3 + chunk], lane.shape),
            jnp.broadcast_to(columns[64:128, 2 + chunk : 3 + chunk], lane.shape),
        ).astype(jnp.int32)
        swapped, flip_a, flip_b = code // 4 % 2 == 1, code // 2 % 2 == 1, code % 2 == 1
        half = lane // 64 * 64
        a = jnp.where(flip_a, 7 - node_a, node_a)
        b = jnp.where(flip_b, 7 - node_b, node_b)
        index_to[chunk] = half + jnp.where(swapped, b * 8 + a, a * 8 + b)
        a = jnp.where(swapped, node_b, node_a)
        b = jnp.where(swapped, node_a, node_b)
        index_from[chunk] = half + jnp.where(flip_a, 7 - a, a) * 8 + jnp.where(flip_b, 7 - b, b)
    scales[...] = jnp.broadcast_to(columns[0:64, 5:6], scales.shape)
    live = (low & (layer > 0)) | ((lane >= 64) & (layer < layers - 1))

    def rows_of(right):
        return slice(right * ELEMENTS, (right + 1) * ELEMENTS)

    def lanes_of(chunk):
        return slice(chunk * LANES, (chunk + 1) * LANES)

    loads[0].wait()
    inverse_h[...], inverse_l[...] = halves(inverse[...])
    loads[1].wait()
    coupling_h[...], coupling_l[...] = halves(coupling[...])
    merged = dot_three(inverse_h[...], inverse_l[...], coupling_h[...], coupling_l[...])
    merged_h[...], merged_l[...] = halves(merged)
    loads[2].wait()
    source_h[...], source_l[...] = halves(source[...])
    image[...] = dot_three(source_h[...], source_l[...], merged_h[...], merged_l[...])

    def to_slots(vector, chunks, stores):
        for chunk in chunks:
            for pair in range(PAIRS):
                left = turned(vector[rows_of(2 * pair), lanes_of(chunk)], index_from[chunk])
                right = turned(vector[rows_of(2 * pair + 1), lanes_of(chunk)], index_from[chunk])
                stores[chunk](pair, *swap_pair(left, right))

    def store_slots(ref):
        def store(pair, even, odd):
            ref[0:64, lanes_of(pair)] = even
            ref[64:128, lanes_of(pair)] = odd

        return store

    def store_ends(pair, even, odd):
        bottoms[rows_of(pair), :] = even
        tops[rows_of(pair), :] = odd

    stores = (store_slots(slots_first), store_slots(slots_second), store_ends)

    def all_peers(ref, sem, width):
        whole = ref.at[pl.ds(0, others * width)]
        return pltpu.make_async_copy(whole, whole, sem)

    def up_copy(phase):
        return pltpu.make_async_remote_copy(
            tops,
            got_bottoms.at[phase],
            up_sem.at[phase, 0],
            up_sem.at[phase, 1],
            device_id={"gz": layer + 1},
            device_id_type=MESH,
        )

    def down_copy(phase):
        return pltpu.make_async_remote_copy(
            bottoms,
            got_tops.at[phase],
            down_sem.at[phase, 0],
            down_sem.at[phase, 1],
            device_id={"gz": layer - 1},
            device_id_type=MESH,
        )

    def start_ends(phase):
        @pl.when(layer < layers - 1)
        def _():
            up_copy(phase).start()

        @pl.when(layer > 0)
        def _():
            down_copy(phase).start()

    def finish_ends(phase):
        @pl.when(layer < layers - 1)
        def _():
            up_copy(phase).wait_send()
            down_copy(phase).wait_recv()

        @pl.when(layer > 0)
        def _():
            down_copy(phase).wait_send()
            up_copy(phase).wait_recv()

    def start_swap(phase, to_holder):
        to_owners = pick(to_owner, slots_second[...])
        to_holders = pick(to_holder, slots_first[...])
        for pair in range(PAIRS):
            sent[phase, pl.ds(pair, blocks, stride=8), :] = to_owners[:, lanes_of(pair)]
            sent[phase, pl.ds(pair + 4, blocks, stride=8), :] = to_holders[:, lanes_of(pair)]

        def send(turn, carry):
            peer = partner(me, turn, blocks)
            pltpu.make_async_remote_copy(
                sent.at[phase, pl.ds(pl.multiple_of(peer * 8, 8), 8)],
                received.at[phase, here],
                swap_sem.at[phase, 0],
                swap_sem.at[phase, 1],
                device_id={"dev": peer},
                device_id_type=MESH,
            ).start()
            return carry

        lax.fori_loop(0, others, send, 0)

    def finish_swap(phase, from_holder):
        nearby_first = pick(near, slots_second[...])
        nearby_second = pick(near_back, slots_first[...])
        all_peers(received.at[phase], swap_sem.at[phase, 1], 8).wait()
        all_peers(sent.at[phase], swap_sem.at[phase, 0], 8).wait()
        finish_ends(phase)
        for pair in range(PAIRS):
            from_owners = received[phase, pl.ds(pair + 4, blocks, stride=8), :]
            from_holders = received[phase, pl.ds(pair, blocks, stride=8), :]
            arrived = (
                nearby_first[:, lanes_of(pair)] + pick(from_holder, from_holders),
                nearby_second[:, lanes_of(pair)] + pick(from_owner, from_owners),
                None,
            )
            for chunk in range(3):
                if chunk < 2:
                    even, odd = arrived[chunk][0:64], arrived[chunk][64:128]
                else:
                    even, odd = got_bottoms[phase, rows_of(pair), :], got_tops[phase, rows_of(pair), :]
                for offset, value in enumerate(swap_pair(even, odd)):
                    yield 2 * pair + offset, chunk, turned(value, index_to[chunk])

    def start_sum(phase, quantities):
        lanes = lane_of((RIGHT, LANES))
        place = row_of((RIGHT, LANES))
        spread = jnp.zeros((RIGHT, LANES), F32)
        for number, rows in enumerate(quantities):
            total = jnp.sum(jnp.concatenate(rows, axis=0), axis=1, keepdims=True)
            spread = jnp.where(lanes == place + number * RIGHT, total, spread)
        mine = jnp.sum(spread, axis=0, keepdims=True)
        sum_out[phase] = mine
        sum_in[phase, me] = mine

        def send(turn, carry):
            pltpu.make_async_remote_copy(
                sum_out.at[phase],
                sum_in.at[phase, me],
                sum_sem.at[phase, 0],
                sum_sem.at[phase, 1],
                device_id={"dev": partner(me, turn, blocks)},
                device_id_type=MESH,
            ).start()
            return carry

        lax.fori_loop(0, others, send, 0)

    def finish_sum(phase, count):
        all_peers(sum_in.at[phase], sum_sem.at[phase, 1], 1).wait()
        all_peers(sum_in.at[phase], sum_sem.at[phase, 0], 1).wait()
        mine = jnp.sum(sum_in[phase], axis=0)
        layer_out[phase] = mine
        layer_in[phase, layer] = mine
        for step in range(1, layers):
            pltpu.make_async_remote_copy(
                layer_out.at[phase],
                layer_in.at[phase, layer],
                layer_sem.at[phase, 0],
                layer_sem.at[phase, 1],
                device_id={"gz": (layer + step) % layers},
                device_id_type=MESH,
            ).start()
        rest = layer_in.at[phase, pl.ds(0, layers - 1)]
        pltpu.make_async_copy(rest, rest, layer_sem.at[phase, 1]).wait()
        pltpu.make_async_copy(rest, rest, layer_sem.at[phase, 0]).wait()
        total = jnp.broadcast_to(jnp.sum(layer_in[phase], axis=0), (RIGHT, LANES))
        lanes = lane_of((RIGHT, LANES))
        place = row_of((RIGHT, LANES))
        return [
            jnp.broadcast_to(
                jnp.sum(
                    jnp.where(lanes == place + number * RIGHT, total, 0.0), axis=1, keepdims=True
                ),
                (RIGHT, LANES),
            )
            for number in range(count)
        ]

    def owned_square(values):
        kept = values[0] * values[0] + jnp.where(low, 0.0, values[2] * values[2])
        return jnp.sum(kept, axis=0, keepdims=True)

    def inner_rows(left, right):
        kept = left[0] * right[0] + left[1] * right[1] + left[2] * right[2]
        return jnp.sum(kept, axis=0, keepdims=True)

    def chunks_of(ref, right):
        return [ref[rows_of(right), lanes_of(chunk)] for chunk in range(3)]

    def scaled_operator():
        return dot_three(vector_h[...], vector_l[...], operator_h[...], operator_l[...])

    def face_values(vector, sides_ref, tops_ref):
        for pair in range(PAIRS):
            for chunk in (0, 2):
                left = turned(vector[rows_of(2 * pair), lanes_of(chunk)], index_from[chunk])
                right = turned(vector[rows_of(2 * pair + 1), lanes_of(chunk)], index_from[chunk])
                even, odd = swap_pair(left, right)
                if chunk == 0:
                    turned_back = jnp.transpose(
                        pick(into_faces, jnp.concatenate([even, odd], axis=0))
                    )
                    target = sides_ref
                else:
                    turned_back = jnp.transpose(odd)
                    target = tops_ref
                for offset in range(2):
                    target[pl.ds(2 * pair + offset, 64, stride=8), :] = turned_back[
                        offset * 64 : (offset + 1) * 64
                    ]

    to_slots(image, (2, 1, 0), stores)
    pl.semaphore_wait(barrier, others + layers - 1)

    def name(turn, carry):
        peer = partner(me, turn, blocks)
        pltpu.make_async_remote_copy(
            named_out.at[peer],
            named_in.at[me],
            named_sem.at[0],
            named_sem.at[1],
            device_id={"dev": peer},
            device_id_type=MESH,
        ).start()
        return carry

    lax.fori_loop(0, others, name, 0)
    start_ends(0)
    solved[...] = dot_three(source_h[...], source_l[...], inverse_h[...], inverse_l[...])
    loads[3].wait()
    operator_h[...], operator_l[...] = halves(operator[...])
    all_peers(named_in, named_sem.at[1], 1).wait()
    all_peers(named_out, named_sem.at[0], 1).wait()
    wanted = named_in[...].reshape(blocks, LANES)
    to_holder_f = onehot(wanted.astype(jnp.int32) == first_row[:blocks] + 1)
    to_holder = to_holder_f.astype(BF16)
    from_holder = jnp.transpose(to_holder_f).astype(BF16)
    start_swap(0, to_holder)

    for right in range(RIGHT):
        for part in range(4):
            solved[rows_of(right), lanes_of(part)] = solved[rows_of(right), lanes_of(part)] / scales[...]
    merged_th[...] = jnp.transpose(merged_h[...].astype(F32)).astype(BF16)
    merged_tl[...] = jnp.transpose(merged_l[...].astype(F32)).astype(BF16)

    for right, chunk, value in finish_swap(0, from_holder):
        value = image[rows_of(right), lanes_of(chunk)] + value
        if chunk == 2:
            value = jnp.where(live, value, 0.0)
        first[rows_of(right), lanes_of(chunk)] = value
        vector_h[rows_of(right), lanes_of(chunk)], vector_l[rows_of(right), lanes_of(chunk)] = halves(value)

    image[...] = scaled_operator()
    squares, curves = [], []
    for right in range(RIGHT):
        for chunk in range(3):
            image[rows_of(right), lanes_of(chunk)] = image[rows_of(right), lanes_of(chunk)] * scales[...]
        mine = chunks_of(first, right)
        squares.append(owned_square(mine))
        curves.append(inner_rows(mine, chunks_of(image, right)))
    start_sum(0, [squares, curves])
    to_slots(image, (2, 1, 0), stores)
    start_ends(1)
    start_swap(1, to_holder)

    moved_zero[...] = dot_three(vector_h[...], vector_l[...], merged_th[...], merged_tl[...])
    face_values(first, sides_zero, tops_zero)
    norm, curve = finish_sum(0, 2)
    alpha = norm / curve

    for right, chunk, value in finish_swap(1, from_holder):
        value = image[rows_of(right), lanes_of(chunk)] + value
        value = first[rows_of(right), lanes_of(chunk)] - alpha[right : right + 1, :] * value
        if chunk == 2:
            value = jnp.where(live, value, 0.0)
        update[rows_of(right), lanes_of(chunk)] = value
        vector_h[rows_of(right), lanes_of(chunk)], vector_l[rows_of(right), lanes_of(chunk)] = halves(value)

    second_image = scaled_operator()
    squares, crosses, curves = [], [], []
    for right in range(RIGHT):
        mine = chunks_of(update, right)
        squares.append(owned_square(mine))
        crosses.append(inner_rows(mine, chunks_of(image, right)))
        scaled = [second_image[rows_of(right), lanes_of(chunk)] * scales[...] for chunk in range(3)]
        curves.append(inner_rows(mine, scaled))
    start_sum(1, [squares, crosses, curves])

    moved_one[...] = dot_three(vector_h[...], vector_l[...], merged_th[...], merged_tl[...])
    face_values(update, sides_one, tops_one)
    norm_next, cross, curve_next = finish_sum(1, 3)
    beta = norm_next / norm
    curve_next = curve_next + 2.0 * beta * cross + beta * beta * curve
    weight_one = norm_next / curve_next
    weight_zero = alpha + weight_one * beta

    writes = []
    for right in range(RIGHT):
        for part in range(4):
            spot = rows_of(right), lanes_of(part)
            solved[spot] = (
                solved[spot]
                - weight_zero[right : right + 1, :] * moved_zero[spot]
                - weight_one[right : right + 1, :] * moved_one[spot]
            )
    writes.append(pltpu.make_async_copy(solved, interior_hbm, store_sem.at[0]))
    writes[-1].start()
    for node in range(64):
        spot = slice(node * 8, node * 8 + 8)
        sides_zero[spot, :] = weight_zero * sides_zero[spot, :] + weight_one * sides_one[spot, :]
        tops_zero[spot, :] = weight_zero[:, :64] * tops_zero[spot, :] + weight_one[:, :64] * tops_one[spot, :]
    writes.append(pltpu.make_async_copy(sides_zero, sides_hbm, store_sem.at[1]))
    writes[-1].start()
    writes.append(pltpu.make_async_copy(tops_zero, tops_hbm, store_sem.at[2]))
    writes[-1].start()
    for write in writes:
        write.wait()


def solution(mesh):
    layers, blocks = mesh.shape["gz"], mesh.shape["dev"]

    def per_device(source, inverse, coupling, operator, face_ids, orientation, scale):
        flat = source.transpose(1, 2, 0).reshape(ROWS, NODES)
        vmem = pltpu.VMEM
        anywhere = pl.BlockSpec(memory_space=pl.ANY)
        local = pl.BlockSpec(memory_space=pltpu.VMEM)
        dma = pltpu.SemaphoreType.DMA
        interior, sides, tops = pl.pallas_call(
            functools.partial(kernel, layers, blocks),
            out_shape=(
                jax.ShapeDtypeStruct((ROWS, NODES), F32),
                jax.ShapeDtypeStruct((512, 128), F32),
                jax.ShapeDtypeStruct((512, 64), F32),
            ),
            in_specs=[anywhere] * 4 + [local] * 3,
            out_specs=(anywhere,) * 3,
            scratch_shapes=[
                vmem((ROWS, NODES), F32),
                vmem((NODES, NODES), F32),
                vmem((NODES, LOCAL), F32),
                vmem((LOCAL, LOCAL), F32),
                *[vmem((ROWS, NODES), BF16)] * 2,
                *[vmem((NODES, NODES), BF16)] * 2,
                *[vmem((NODES, LOCAL), BF16)] * 2,
                *[vmem((LOCAL, LOCAL), BF16)] * 2,
                *[vmem((NODES, LOCAL), BF16)] * 2,
                *[vmem((LOCAL, NODES), BF16)] * 2,
                vmem((LANES, LANES), F32),
                vmem((3, ELEMENTS, LANES), jnp.int32),
                vmem((3, ELEMENTS, LANES), jnp.int32),
                vmem((ELEMENTS, LANES), F32),
                *[vmem((ROWS, LOCAL), F32)] * 3,
                *[vmem((ROWS, LOCAL), BF16)] * 2,
                *[vmem((128, 512), F32)] * 2,
                *[vmem((256, 128), F32)] * 2,
                *[vmem((ROWS, NODES), F32)] * 3,
                *[vmem((512, 128), F32)] * 2,
                *[vmem((512, 64), F32)] * 2,
                *[vmem((blocks, 1, LANES), F32)] * 2,
                *[vmem((2, blocks * 8, LANES), F32)] * 2,
                *[vmem((2, 256, 128), F32)] * 2,
                vmem((2, 1, LANES), F32),
                vmem((2, blocks, 1, LANES), F32),
                vmem((2, 1, LANES), F32),
                vmem((2, layers, 1, LANES), F32),
                dma((4,)),
                dma((3,)),
                dma((2,)),
                dma((2, 2)),
                dma((2, 2)),
                dma((2, 2)),
                dma((2, 2)),
                dma((2, 2)),
            ],
            compiler_params=pltpu.CompilerParams(collective_id=0, has_side_effects=True),
        )(
            flat,
            inverse,
            coupling,
            operator,
            face_ids.T,
            orientation.T,
            scale.reshape(1, ELEMENTS),
        )
        return (
            interior.reshape(RIGHT, ELEMENTS, NODES).transpose(2, 0, 1),
            sides.reshape(64, RIGHT, 128),
            tops.reshape(64, RIGHT, ELEMENTS),
        )

    columns = P(None, None, ("gz", "dev"))
    return jax.shard_map(
        per_device,
        mesh=mesh,
        in_specs=(
            columns,
            P(),
            P(),
            P(),
            P(("gz", "dev"), None),
            P(("gz", "dev"), None),
            P(("gz", "dev")),
        ),
        out_specs=(columns, columns, columns),
        check_vma=False,
    )
```

profile of v0, /device:TPU:1, one launch (start us, length us, event | category | flops | bytes accessed | tf_op | source)
XLA Modules:
  0.0 65.0 jit_solution(5989487994265808736)
XLA Ops:
  0.6 60.3 %shard_map.94 = (f32[512,512]{1,0:T(8,128)}, f32[512,128]{1,0:T(8,128)}, f32[512,64]{1,0:T(8,128)}) custom-call(f32[512,512]{1,0:T(8,128)} %bitcast.11, f32[512,512]{1,0:T(8,128)} %inverse_hbm.1, f32[512,384]{1,0:T(8,128)} %coupling_hbm.1, f32[384,384]{1,0:T(8,128)} %operator_hbm.1, s32[4,64]{1,0:T(4,128)} %bitcast.16, s32[6,64]{1,0:T(8,128)} %bitcast.15, ...), custom_call_target="tpu_custom_call" | custom-call | tf_op jit(solution)/shard_map/pallas_call | solution.py:563
  60.9 0.0 copy-start.1
  60.9 2.3 %copy.13 = f32[512,8,64]{0,2,1:T(8,128)} copy(f32[512,8,64]{0,2,1:T(8,128)} %bitcast.12) | data formatting | bytes 2097152
  63.2 0.0 copy-done.1
  63.2 0.0 copy-start
  63.2 0.7 %copy.14 = f32[64,8,128]{2,1,0:T(8,128)} copy(f32[64,8,128]{2,1,0:T(8,128)S(1)} %bitcast.14) | data formatting | bytes 524288
  63.9 0.3 copy-done
  64.3 0.7 %copy.15 = f32[64,8,64]{2,1,0:T(8,128)} copy(f32[64,8,64]{2,1,0:T(8,128)S(1)} %bitcast.13) | data formatting | bytes 262144
Async XLA Ops:
  60.9 2.3 %copy-start.1 = (f32[512,128]{1,0:T(8,128)S(1)}, f32[512,128]{1,0:T(8,128)}, u32[]{:S(2)}) copy-start(f32[512,128]{1,0:T(8,128)} %get-tuple-element.7) | copy-start | bytes 786436
  63.2 1.0 %copy-start = (f32[512,64]{1,0:T(8,128)S(1)}, f32[512,64]{1,0:T(8,128)}, u32[]{:S(2)}) copy-start(f32[512,64]{1,0:T(8,128)} %get-tuple-element.8) | copy-start | bytes 393220
where the time goes:
time: 65.2 us; the launch traced here: 65 us
  Pallas kernels  60.3 us (92%)
  local copies, waits for them, and re-layouts  4.05 us (6%)
    pallas_call x1, Pallas kernels, per_device(): pl.pallas_call(functools.partial(kernel, layers, blocks), out_shape=(jax....  60.3 us
    unnamed x7, local copies, waits for them, and re-layouts  4.05 us

commit v1 on v0

--- a/solution.py
+++ b/solution.py
@@ -76,16 +76,24 @@
     inverse_hbm,
     coupling_hbm,
     operator_hbm,
-    faces_ref,
-    codes_ref,
-    scale_ref,
-    interior_hbm,
-    sides_hbm,
-    tops_hbm,
+    faces_hbm,
+    codes_hbm,
+    scale_hbm,
+    solved,
+    moved_zero,
+    moved_one,
+    sides_zero,
+    sides_one,
+    tops_zero,
+    tops_one,
+    weights,
     source,
     inverse,
     coupling,
     operator,
+    faces_ref,
+    codes_ref,
+    scale_ref,
     source_h,
     source_l,
     inverse_h,
@@ -111,35 +119,27 @@
     slots_second,
     bottoms,
     tops,
-    solved,
-    moved_zero,
-    moved_one,
-    sides_zero,
-    sides_one,
-    tops_zero,
-    tops_one,
-    named_out,
-    named_in,
+    second_image,
     sent,
     received,
     got_bottoms,
     got_tops,
-    sum_out,
-    sum_in,
-    layer_out,
-    layer_in,
+    near_out,
+    near_in,
+    far_out,
+    far_in,
     load_sem,
-    store_sem,
-    named_sem,
     swap_sem,
     up_sem,
     down_sem,
-    sum_sem,
-    layer_sem,
+    near_sem,
+    far_sem,
 ):
     layer = lax.axis_index("gz")
     me = lax.axis_index("dev")
     others = blocks - 1
+    core = me % 2
+    core_pair = me // 2 * 2
 
     barrier = pltpu.get_barrier_semaphore()
 
@@ -151,23 +151,29 @@
 
     lax.fori_loop(0, others, greet, 0)
     for step in range(1, layers):
-        pl.semaphore_signal(
-            barrier, inc=1, device_id={"gz": (layer + step) % layers}, device_id_type=MESH
-        )
+        for side in range(2):
+            pl.semaphore_signal(
+                barrier,
+                inc=1,
+                device_id=((layer + step) % layers, core_pair + (core + side) % 2),
+                device_id_type=MESH,
+            )
 
     loads = [
         pltpu.make_async_copy(inverse_hbm, inverse, load_sem.at[0]),
         pltpu.make_async_copy(coupling_hbm, coupling, load_sem.at[1]),
         pltpu.make_async_copy(source_hbm, source, load_sem.at[2]),
         pltpu.make_async_copy(operator_hbm, operator, load_sem.at[3]),
+        pltpu.make_async_copy(faces_hbm, faces_ref, load_sem.at[4]),
+        pltpu.make_async_copy(codes_hbm, codes_ref, load_sem.at[5]),
+        pltpu.make_async_copy(scale_hbm, scale_ref, load_sem.at[6]),
     ]
-    for load in loads:
+    for load in loads[4:] + loads[:4]:
         load.start()
 
     here = pl.ds(pl.multiple_of(me * 8, 8), 8)
-    for phase in range(2):
+    for phase in range(3):
         received[phase, here, :] = jnp.zeros((8, LANES), F32)
-    named_in[me] = jnp.zeros((1, LANES), F32)
 
     @pl.when(layer == 0)
     def _():
@@ -178,6 +184,8 @@
         got_tops[...] = jnp.zeros(got_tops.shape, F32)
 
     table[...] = jnp.zeros(table.shape, F32)
+    for load in loads[4:]:
+        load.wait()
     faces = faces_ref[...].astype(F32)
     codes = codes_ref[...].astype(F32)
     for row in range(2):
@@ -208,9 +216,7 @@
     from_owner = jnp.transpose(to_owner_f).astype(BF16)
     slot_number = (second_row[:blocks] % LANES + 1).astype(F32)
     named = jnp.sum(to_owner_f * slot_number, axis=1, keepdims=True)
-    named = jnp.broadcast_to(named, peers)
-    for peer in range(blocks):
-        named_out[peer] = named[peer : peer + 1, :]
+    sent[0, pl.ds(4, blocks, stride=8), :] = jnp.broadcast_to(named, peers)
 
     lane = lane_of((ELEMENTS, LANES))
     low = lane < 64
@@ -268,9 +274,9 @@
 
     stores = (store_slots(slots_first), store_slots(slots_second), store_ends)
 
-    def all_peers(ref, sem, width):
-        whole = ref.at[pl.ds(0, others * width)]
-        return pltpu.make_async_copy(whole, whole, sem)
+    def wait_rows(ref, rows, sem):
+        whole = ref.at[pl.ds(0, rows)]
+        pltpu.make_async_copy(whole, whole, sem).wait()
 
     def up_copy(phase):
         return pltpu.make_async_remote_copy(
@@ -312,18 +318,12 @@
             down_copy(phase).wait_send()
             up_copy(phase).wait_recv()
 
-    def start_swap(phase, to_holder):
-        to_owners = pick(to_owner, slots_second[...])
-        to_holders = pick(to_holder, slots_first[...])
-        for pair in range(PAIRS):
-            sent[phase, pl.ds(pair, blocks, stride=8), :] = to_owners[:, lanes_of(pair)]
-            sent[phase, pl.ds(pair + 4, blocks, stride=8), :] = to_holders[:, lanes_of(pair)]
-
+    def send_rows(phase, rows):
         def send(turn, carry):
             peer = partner(me, turn, blocks)
             pltpu.make_async_remote_copy(
-                sent.at[phase, pl.ds(pl.multiple_of(peer * 8, 8), 8)],
-                received.at[phase, here],
+                sent.at[phase, pl.ds(pl.multiple_of(peer * 8, 8), rows)],
+                received.at[phase, pl.ds(pl.multiple_of(me * 8, 8), rows)],
                 swap_sem.at[phase, 0],
                 swap_sem.at[phase, 1],
                 device_id={"dev": peer},
@@ -333,27 +333,42 @@
 
         lax.fori_loop(0, others, send, 0)
 
-    def finish_swap(phase, from_holder):
-        nearby_first = pick(near, slots_second[...])
-        nearby_second = pick(near_back, slots_first[...])
-        all_peers(received.at[phase], swap_sem.at[phase, 1], 8).wait()
-        all_peers(sent.at[phase], swap_sem.at[phase, 0], 8).wait()
-        finish_ends(phase)
+    def wait_sent(phase, rows):
+        wait_rows(sent.at[phase], others * rows, swap_sem.at[phase, 0])
+
+    def wait_received(phase, rows):
+        wait_rows(received.at[phase], others * rows, swap_sem.at[phase, 1])
+
+    def put(phase, first_row, value):
         for pair in range(PAIRS):
-            from_owners = received[phase, pl.ds(pair + 4, blocks, stride=8), :]
-            from_holders = received[phase, pl.ds(pair, blocks, stride=8), :]
-            arrived = (
-                nearby_first[:, lanes_of(pair)] + pick(from_holder, from_holders),
-                nearby_second[:, lanes_of(pair)] + pick(from_owner, from_owners),
-                None,
-            )
-            for chunk in range(3):
-                if chunk < 2:
-                    even, odd = arrived[chunk][0:64], arrived[chunk][64:128]
-                else:
-                    even, odd = got_bottoms[phase, rows_of(pair), :], got_tops[phase, rows_of(pair), :]
-                for offset, value in enumerate(swap_pair(even, odd)):
-                    yield 2 * pair + offset, chunk, turned(value, index_to[chunk])
+            sent[phase, pl.ds(first_row + pair, blocks, stride=8), :] = value[:, lanes_of(pair)]
+
+    def got(phase, row):
+        return received[phase, pl.ds(row, blocks, stride=8), :]
+
+    def arrivals(chunk, pair, value):
+        for offset, part in enumerate(swap_pair(value[0:64], value[64:128])):
+            yield 2 * pair + offset, turned(part, index_to[chunk])
+
+    def end_arrivals(phase):
+        for pair in range(PAIRS):
+            ends = got_bottoms[phase, rows_of(pair), :], got_tops[phase, rows_of(pair), :]
+            for right, part in arrivals(2, pair, jnp.concatenate(ends, axis=0)):
+                spot = rows_of(right), lanes_of(2)
+                yield spot, jnp.where(live, image[spot] + part, 0.0)
+
+    def keep(ref, spot, value):
+        ref[spot] = value
+        vector_h[spot], vector_l[spot] = halves(value)
+
+    def sum_peer(turn):
+        step = (layers // 2 + (turn // 2 + 1) // 2 * (1 - 2 * (turn // 2 % 2))) % layers
+        return (layer + step) % layers, core_pair + (core + 1 - turn % 2) % 2
+
+    def far_peer(turn):
+        if blocks == 64:
+            return partner(me, 2 * turn + 1, blocks)
+        return (me + 2 * (turn + 1)) % blocks
 
     def start_sum(phase, quantities):
         lanes = lane_of((RIGHT, LANES))
@@ -363,41 +378,46 @@
             total = jnp.sum(jnp.concatenate(rows, axis=0), axis=1, keepdims=True)
             spread = jnp.where(lanes == place + number * RIGHT, total, spread)
         mine = jnp.sum(spread, axis=0, keepdims=True)
-        sum_out[phase] = mine
-        sum_in[phase, me] = mine
+        near_out[phase] = mine
+        near_in[phase, layer * 2 + core] = mine
 
         def send(turn, carry):
             pltpu.make_async_remote_copy(
-                sum_out.at[phase],
-                sum_in.at[phase, me],
-                sum_sem.at[phase, 0],
-                sum_sem.at[phase, 1],
-                device_id={"dev": partner(me, turn, blocks)},
+                near_out.at[phase],
+                near_in.at[phase, layer * 2 + core],
+                near_sem.at[phase, 0],
+                near_sem.at[phase, 1],
+                device_id=sum_peer(turn),
                 device_id_type=MESH,
             ).start()
             return carry
 
-        lax.fori_loop(0, others, send, 0)
-
-    def finish_sum(phase, count):
-        all_peers(sum_in.at[phase], sum_sem.at[phase, 1], 1).wait()
-        all_peers(sum_in.at[phase], sum_sem.at[phase, 0], 1).wait()
-        mine = jnp.sum(sum_in[phase], axis=0)
-        layer_out[phase] = mine
-        layer_in[phase, layer] = mine
-        for step in range(1, layers):
+        lax.fori_loop(0, 2 * layers - 1, send, 0)
+
+    def middle_sum(phase):
+        wait_rows(near_in.at[phase], 2 * layers - 1, near_sem.at[phase, 1])
+        wait_rows(near_in.at[phase], 2 * layers - 1, near_sem.at[phase, 0])
+        mine = jnp.sum(near_in[phase], axis=0)
+        far_out[phase] = mine
+        far_in[phase, me // 2] = mine
+
+        def send(turn, carry):
             pltpu.make_async_remote_copy(
-                layer_out.at[phase],
-                layer_in.at[phase, layer],
-                layer_sem.at[phase, 0],
-                layer_sem.at[phase, 1],
-                device_id={"gz": (layer + step) % layers},
+                far_out.at[phase],
+                far_in.at[phase, me // 2],
+                far_sem.at[phase, 0],
+                far_sem.at[phase, 1],
+                device_id={"dev": far_peer(turn)},
                 device_id_type=MESH,
             ).start()
-        rest = layer_in.at[phase, pl.ds(0, layers - 1)]
-        pltpu.make_async_copy(rest, rest, layer_sem.at[phase, 1]).wait()
-        pltpu.make_async_copy(rest, rest, layer_sem.at[phase, 0]).wait()
-        total = jnp.broadcast_to(jnp.sum(layer_in[phase], axis=0), (RIGHT, LANES))
+            return carry
+
+        lax.fori_loop(0, blocks // 2 - 1, send, 0)
+
+    def finish_sum(phase, count):
+        wait_rows(far_in.at[phase], blocks // 2 - 1, far_sem.at[phase, 1])
+        wait_rows(far_in.at[phase], blocks // 2 - 1, far_sem.at[phase, 0])
+        total = jnp.broadcast_to(jnp.sum(far_in[phase], axis=0), (RIGHT, LANES))
         lanes = lane_of((RIGHT, LANES))
         place = row_of((RIGHT, LANES))
         return [
@@ -421,8 +441,16 @@
     def chunks_of(ref, right):
         return [ref[rows_of(right), lanes_of(chunk)] for chunk in range(3)]
 
-    def scaled_operator():
-        return dot_three(vector_h[...], vector_l[...], operator_h[...], operator_l[...])
+    def operated(chunks):
+        return sum(
+            dot_three(
+                vector_h[:, lanes_of(chunk)],
+                vector_l[:, lanes_of(chunk)],
+                operator_h[lanes_of(chunk), :],
+                operator_l[lanes_of(chunk), :],
+            )
+            for chunk in chunks
+        )
 
     def face_values(vector, sides_ref, tops_ref):
         for pair in range(PAIRS):
@@ -444,47 +472,40 @@
                     ]
 
     to_slots(image, (2, 1, 0), stores)
-    pl.semaphore_wait(barrier, others + layers - 1)
-
-    def name(turn, carry):
-        peer = partner(me, turn, blocks)
-        pltpu.make_async_remote_copy(
-            named_out.at[peer],
-            named_in.at[me],
-            named_sem.at[0],
-            named_sem.at[1],
-            device_id={"dev": peer},
-            device_id_type=MESH,
-        ).start()
-        return carry
-
-    lax.fori_loop(0, others, name, 0)
+    put(0, 0, pick(to_owner, slots_second[...]))
+    pl.semaphore_wait(barrier, others + 2 * (layers - 1))
+
+    send_rows(0, 5)
     start_ends(0)
     solved[...] = dot_three(source_h[...], source_l[...], inverse_h[...], inverse_l[...])
     loads[3].wait()
     operator_h[...], operator_l[...] = halves(operator[...])
-    all_peers(named_in, named_sem.at[1], 1).wait()
-    all_peers(named_out, named_sem.at[0], 1).wait()
-    wanted = named_in[...].reshape(blocks, LANES)
-    to_holder_f = onehot(wanted.astype(jnp.int32) == first_row[:blocks] + 1)
+    nearby_first = pick(near, slots_second[...])
+    wait_received(0, 5)
+    to_holder_f = onehot(got(0, 4).astype(jnp.int32) == first_row[:blocks] + 1)
     to_holder = to_holder_f.astype(BF16)
     from_holder = jnp.transpose(to_holder_f).astype(BF16)
-    start_swap(0, to_holder)
-
-    for right in range(RIGHT):
-        for part in range(4):
-            solved[rows_of(right), lanes_of(part)] = solved[rows_of(right), lanes_of(part)] / scales[...]
-    merged_th[...] = jnp.transpose(merged_h[...].astype(F32)).astype(BF16)
-    merged_tl[...] = jnp.transpose(merged_l[...].astype(F32)).astype(BF16)
-
-    for right, chunk, value in finish_swap(0, from_holder):
-        value = image[rows_of(right), lanes_of(chunk)] + value
-        if chunk == 2:
-            value = jnp.where(live, value, 0.0)
-        first[rows_of(right), lanes_of(chunk)] = value
-        vector_h[rows_of(right), lanes_of(chunk)], vector_l[rows_of(right), lanes_of(chunk)] = halves(value)
-
-    image[...] = scaled_operator()
+
+    put(1, 0, pick(to_holder, slots_first[...]))
+    send_rows(1, 4)
+    for pair in range(PAIRS):
+        value = nearby_first[:, lanes_of(pair)] + pick(from_holder, got(0, pair))
+        for right, part in arrivals(0, pair, value):
+            spot = rows_of(right), lanes_of(0)
+            keep(first, spot, image[spot] + part)
+    finish_ends(0)
+    for spot, value in end_arrivals(0):
+        keep(first, spot, value)
+    second_image[...] = operated((0, 2))
+    nearby_second = pick(near_back, slots_first[...])
+    wait_received(1, 4)
+    for pair in range(PAIRS):
+        value = nearby_second[:, lanes_of(pair)] + pick(from_owner, got(1, pair))
+        for right, part in arrivals(1, pair, value):
+            spot = rows_of(right), lanes_of(1)
+            keep(first, spot, image[spot] + part)
+    image[...] = second_image[...] + operated((1,))
+
     squares, curves = [], []
     for right in range(RIGHT):
         for chunk in range(3):
@@ -493,62 +514,78 @@
         squares.append(owned_square(mine))
         curves.append(inner_rows(mine, chunks_of(image, right)))
     start_sum(0, [squares, curves])
-    to_slots(image, (2, 1, 0), stores)
+    wait_sent(0, 5)
+    wait_sent(1, 4)
+    to_slots(image, (1, 0, 2), stores)
+    put(2, 0, pick(to_owner, slots_second[...]))
+    put(2, 4, pick(to_holder, slots_first[...]))
+    send_rows(2, 8)
     start_ends(1)
-    start_swap(1, to_holder)
-
+
+    middle_sum(0)
+    nearby_first = pick(near, slots_second[...])
+    nearby_second = pick(near_back, slots_first[...])
+    for right in range(RIGHT):
+        for part in range(4):
+            solved[rows_of(right), lanes_of(part)] = solved[rows_of(right), lanes_of(part)] / scales[...]
+    merged_th[...] = jnp.transpose(merged_h[...].astype(F32)).astype(BF16)
+    merged_tl[...] = jnp.transpose(merged_l[...].astype(F32)).astype(BF16)
     moved_zero[...] = dot_three(vector_h[...], vector_l[...], merged_th[...], merged_tl[...])
     face_values(first, sides_zero, tops_zero)
+    finish_ends(1)
+    for spot, value in end_arrivals(1):
+        keep(update, spot, value)
+    wait_received(2, 8)
+    wait_sent(2, 8)
+    for pair in range(PAIRS):
+        arrived = (
+            nearby_first[:, lanes_of(pair)] + pick(from_holder, got(2, pair)),
+            nearby_second[:, lanes_of(pair)] + pick(from_owner, got(2, pair + 4)),
+        )
+        for chunk in range(2):
+            for right, part in arrivals(chunk, pair, arrived[chunk]):
+                spot = rows_of(right), lanes_of(chunk)
+                keep(update, spot, image[spot] + part)
+    second_image[...] = operated((0, 1, 2))
+
     norm, curve = finish_sum(0, 2)
     alpha = norm / curve
-
-    for right, chunk, value in finish_swap(1, from_holder):
-        value = image[rows_of(right), lanes_of(chunk)] + value
-        value = first[rows_of(right), lanes_of(chunk)] - alpha[right : right + 1, :] * value
-        if chunk == 2:
-            value = jnp.where(live, value, 0.0)
-        update[rows_of(right), lanes_of(chunk)] = value
-        vector_h[rows_of(right), lanes_of(chunk)], vector_l[rows_of(right), lanes_of(chunk)] = halves(value)
-
-    second_image = scaled_operator()
     squares, crosses, curves = [], [], []
     for right in range(RIGHT):
-        mine = chunks_of(update, right)
+        step = alpha[right : right + 1, :]
+        before, change = chunks_of(first, right), chunks_of(update, right)
+        old, turned_change = chunks_of(image, right), chunks_of(second_image, right)
+        mine = [before[chunk] - step * change[chunk] for chunk in range(3)]
+        new = [old[chunk] - step * (turned_change[chunk] * scales[...]) for chunk in range(3)]
         squares.append(owned_square(mine))
-        crosses.append(inner_rows(mine, chunks_of(image, right)))
-        scaled = [second_image[rows_of(right), lanes_of(chunk)] * scales[...] for chunk in range(3)]
-        curves.append(inner_rows(mine, scaled))
+        crosses.append(inner_rows(mine, old))
+        curves.append(inner_rows(mine, new))
     start_sum(1, [squares, crosses, curves])
 
     moved_one[...] = dot_three(vector_h[...], vector_l[...], merged_th[...], merged_tl[...])
+    middle_sum(1)
     face_values(update, sides_one, tops_one)
     norm_next, cross, curve_next = finish_sum(1, 3)
     beta = norm_next / norm
     curve_next = curve_next + 2.0 * beta * cross + beta * beta * curve
-    weight_one = norm_next / curve_next
-    weight_zero = alpha + weight_one * beta
-
-    writes = []
+    weight_update = norm_next / curve_next
+    weights[0:8, :] = alpha + weight_update * beta + weight_update
+    weights[8:16, :] = weight_update * alpha
+
+
+def combine(weights, solved, moved_zero, moved_one, sides_zero, sides_one, tops_zero, tops_one, interior, sides, tops):
     for right in range(RIGHT):
         for part in range(4):
-            spot = rows_of(right), lanes_of(part)
-            solved[spot] = (
+            spot = slice(right * 64, right * 64 + 64), slice(part * LANES, part * LANES + LANES)
+            interior[spot] = (
                 solved[spot]
-                - weight_zero[right : right + 1, :] * moved_zero[spot]
-                - weight_one[right : right + 1, :] * moved_one[spot]
+                - weights[right : right + 1, :] * moved_zero[spot]
+                + weights[8 + right : 9 + right, :] * moved_one[spot]
             )
-    writes.append(pltpu.make_async_copy(solved, interior_hbm, store_sem.at[0]))
-    writes[-1].start()
     for node in range(64):
         spot = slice(node * 8, node * 8 + 8)
-        sides_zero[spot, :] = weight_zero * sides_zero[spot, :] + weight_one * sides_one[spot, :]
-        tops_zero[spot, :] = weight_zero[:, :64] * tops_zero[spot, :] + weight_one[:, :64] * tops_one[spot, :]
-    writes.append(pltpu.make_async_copy(sides_zero, sides_hbm, store_sem.at[1]))
-    writes[-1].start()
-    writes.append(pltpu.make_async_copy(tops_zero, tops_hbm, store_sem.at[2]))
-    writes[-1].start()
-    for write in writes:
-        write.wait()
+        sides[spot, :] = weights[0:8, :] * sides_zero[spot, :] - weights[8:16, :] * sides_one[spot, :]
+        tops[spot, :] = weights[0:8, :64] * tops_zero[spot, :] - weights[8:16, :64] * tops_one[spot, :]
 
 
 def solution(mesh):
@@ -557,23 +594,28 @@
     def per_device(source, inverse, coupling, operator, face_ids, orientation, scale):
         flat = source.transpose(1, 2, 0).reshape(ROWS, NODES)
         vmem = pltpu.VMEM
-        anywhere = pl.BlockSpec(memory_space=pl.ANY)
+        far = pl.BlockSpec(memory_space=pltpu.HBM)
         local = pl.BlockSpec(memory_space=pltpu.VMEM)
         dma = pltpu.SemaphoreType.DMA
-        interior, sides, tops = pl.pallas_call(
+        shapes = [
+            *[jax.ShapeDtypeStruct((ROWS, NODES), F32)] * 3,
+            *[jax.ShapeDtypeStruct((512, 128), F32)] * 2,
+            *[jax.ShapeDtypeStruct((512, 64), F32)] * 2,
+            jax.ShapeDtypeStruct((16, LANES), F32),
+        ]
+        *found, weights = pl.pallas_call(
             functools.partial(kernel, layers, blocks),
-            out_shape=(
-                jax.ShapeDtypeStruct((ROWS, NODES), F32),
-                jax.ShapeDtypeStruct((512, 128), F32),
-                jax.ShapeDtypeStruct((512, 64), F32),
-            ),
-            in_specs=[anywhere] * 4 + [local] * 3,
-            out_specs=(anywhere,) * 3,
+            out_shape=tuple(shapes),
+            in_specs=[far] * 7,
+            out_specs=(local,) * 8,
             scratch_shapes=[
                 vmem((ROWS, NODES), F32),
                 vmem((NODES, NODES), F32),
                 vmem((NODES, LOCAL), F32),
                 vmem((LOCAL, LOCAL), F32),
+                vmem((4, ELEMENTS), jnp.int32),
+                vmem((6, ELEMENTS), jnp.int32),
+                vmem((1, ELEMENTS), jnp.int32),
                 *[vmem((ROWS, NODES), BF16)] * 2,
                 *[vmem((NODES, NODES), BF16)] * 2,
                 *[vmem((NODES, LOCAL), BF16)] * 2,
@@ -588,26 +630,23 @@
                 *[vmem((ROWS, LOCAL), BF16)] * 2,
                 *[vmem((128, 512), F32)] * 2,
                 *[vmem((256, 128), F32)] * 2,
-                *[vmem((ROWS, NODES), F32)] * 3,
-                *[vmem((512, 128), F32)] * 2,
-                *[vmem((512, 64), F32)] * 2,
-                *[vmem((blocks, 1, LANES), F32)] * 2,
-                *[vmem((2, blocks * 8, LANES), F32)] * 2,
+                vmem((ROWS, LOCAL), F32),
+                *[vmem((3, blocks * 8, LANES), F32)] * 2,
                 *[vmem((2, 256, 128), F32)] * 2,
                 vmem((2, 1, LANES), F32),
-                vmem((2, blocks, 1, LANES), F32),
+                vmem((2, 2 * layers, 1, LANES), F32),
                 vmem((2, 1, LANES), F32),
-                vmem((2, layers, 1, LANES), F32),
-                dma((4,)),
-                dma((3,)),
-                dma((2,)),
-                dma((2, 2)),
+                vmem((2, blocks // 2, 1, LANES), F32),
+                dma((7,)),
+                dma((3, 2)),
                 dma((2, 2)),
                 dma((2, 2)),
                 dma((2, 2)),
                 dma((2, 2)),
             ],
-            compiler_params=pltpu.CompilerParams(collective_id=0, has_side_effects=True),
+            compiler_params=pltpu.CompilerParams(
+                collective_id=0, has_side_effects=True, vmem_limit_bytes=32 << 20
+            ),
         )(
             flat,
             inverse,
@@ -617,6 +656,13 @@
             orientation.T,
             scale.reshape(1, ELEMENTS),
         )
+        interior, sides, tops = pl.pallas_call(
+            combine,
+            out_shape=(shapes[0], shapes[3], shapes[5]),
+            in_specs=[local] * 8,
+            out_specs=(local,) * 3,
+            compiler_params=pltpu.CompilerParams(vmem_limit_bytes=16 << 20),
+        )(weights, *found)
         return (
             interior.reshape(RIGHT, ELEMENTS, NODES).transpose(2, 0, 1),
             sides.reshape(64, RIGHT, 128),

time: 65.2 us -> 60 us (0.920)
  Pallas kernels: 60.3 us -> 53.8 us
  local copies, waits for them, and re-layouts: 4.05 us -> 5.32 us
    pallas_call x1 -> x2, Pallas kernels: 60.3 us -> 53.8 us  [the longest x1 52.4 us: per_device(): pl.pallas_call(functools.partial(kernel, layers, blocks), out_shape=tuple...]
    unnamed x7 -> x14, local copies, waits for them, and re-layouts: 4.05 us -> 5.32 us
where the time goes in v1:
time: 60 us; the launch traced here: 59.8 us
  Pallas kernels  53.8 us (90%)
  local copies, waits for them, and re-layouts  5.32 us (9%)
  between operations  0.67 us (1%)
    pallas_call x1, Pallas kernels, per_device(): pl.pallas_call(functools.partial(kernel, layers, blocks), out_shape=tuple...  52.4 us
    unnamed x14, local copies, waits for them, and re-layouts  5.32 us
    pallas_call x1, Pallas kernels, per_device(): pl.pallas_call(combine, out_shape=(shapes[0], shapes[3], shapes[5]), in_s...  1.35 us

profile of v1, /device:TPU:1, one launch (start us, length us, event | category | flops | bytes accessed | tf_op | source)
XLA Modules:
  0.0 59.8 jit_solution(1732804753180088466)
XLA Ops:
  0.6 0.0 copy-start.4
  0.6 0.0 copy-start.5
  0.7 0.0 copy-start.6
  0.7 0.7 %copy-done.4 = s32[64,6]{0,1:T(8,128)S(1)} copy-done((s32[64,6]{0,1:T(8,128)S(1)}, s32[64,6]{0,1:T(8,128)}, u32[]{:S(2)}) %copy-start.4) | copy-done | bytes 1560
  1.3 0.0 copy-done.5
  1.3 0.0 copy-done.6
  1.3 0.0 copy-start
  1.3 1.2 %copy-done = f32[512,8,64]{0,2,1:T(8,128)S(1)} copy-done((f32[512,8,64]{0,2,1:T(8,128)S(1)}, f32[512,8,64]{0,2,1:T(8,128)}, u32[]{:S(2)}) %copy-start) | copy-done | bytes 1048600
  2.6 0.0 copy-start.1
  2.6 1.2 %copy-done.1 = f32[512,512]{1,0:T(8,128)S(1)} copy-done((f32[512,512]{1,0:T(8,128)S(1)}, f32[512,512]{1,0:T(8,128)}, u32[]{:S(2)}) %copy-start.1) | copy-done | bytes 1048600
  3.8 0.0 copy-start.2
  3.8 1.1 %copy-done.2 = f32[512,384]{1,0:T(8,128)S(1)} copy-done((f32[512,384]{1,0:T(8,128)S(1)}, f32[512,384]{1,0:T(8,128)}, u32[]{:S(2)}) %copy-start.2) | copy-done | bytes 786456
  4.9 0.0 copy-start.3
  4.9 1.1 %copy-done.3 = f32[384,384]{1,0:T(8,128)S(1)} copy-done((f32[384,384]{1,0:T(8,128)S(1)}, f32[384,384]{1,0:T(8,128)}, u32[]{:S(2)}) %copy-start.3) | copy-done | bytes 589848
  6.0 52.4 %shard_map.94 = (f32[512,512]{1,0:T(8,128)S(1)}, f32[512,512]{1,0:T(8,128)S(1)}, f32[512,512]{1,0:T(8,128)S(1)}, f32[512,128]{1,0:T(8,128)S(1)}, f32[512,128]{1,...) custom-call(f32[512,512]{1,0:T(8,128)S(1)} %bitcast.11, ...), custom_call_target="tpu_custom_call" | custom-call | tf_op jit(solution)/shard_map/pallas_call | solution.py:606
  58.4 1.3 %shard_map.95 = (f32[512,512]{1,0:T(8,128)}, f32[512,128]{1,0:T(8,128)}, f32[512,64]{1,0:T(8,128)}) custom-call(f32[16,128]{1,0:T(8,128)S(1)} %get-tuple-element.14.weights, f32[512,512]{1,0:T(8,128)S(1)} %get-tuple-element.15.solved, f32[512,512]{1,0:T(8,128)S(1)} %get-tuple-element.16.moved_zero, f32[512,512]{1,0:T(8,128)S(1)} %get-tuple-element.17.moved_one, ...), custom_call_target="tpu_custom_call" | custom-call | tf_op jit(solution)/shard_map/pallas_call | solution.py:659
Async XLA Ops:
  0.6 0.7 %copy-start.4 = (s32[64,6]{0,1:T(8,128)S(1)}, s32[64,6]{0,1:T(8,128)}, u32[]{:S(2)}) copy-start(s32[64,6]{0,1:T(8,128)} %param.12) | copy-start | bytes 4612
  0.6 0.7 %copy-start.5 = (s32[64,4]{0,1:T(4,128)S(1)}, s32[64,4]{0,1:T(4,128)}, u32[]{:S(2)}) copy-start(s32[64,4]{0,1:T(4,128)} %param.11) | copy-start | bytes 3076
  0.7 0.7 %copy-start.6 = (s32[64]{0:T(128)S(1)}, s32[64]{0:T(128)}, u32[]{:S(2)}) copy-start(s32[64]{0:T(128)} %param.13) | copy-start | bytes 772
  1.3 1.2 %copy-start = (f32[512,8,64]{0,2,1:T(8,128)S(1)}, f32[512,8,64]{0,2,1:T(8,128)}, u32[]{:S(2)}) copy-start(f32[512,8,64]{0,2,1:T(8,128)} %param.7) | copy-start | bytes 3145732
  2.6 1.2 %copy-start.1 = (f32[512,512]{1,0:T(8,128)S(1)}, f32[512,512]{1,0:T(8,128)}, u32[]{:S(2)}) copy-start(f32[512,512]{1,0:T(8,128)} %inverse_hbm.1) | copy-start | bytes 3145732
  3.8 1.1 %copy-start.2 = (f32[512,384]{1,0:T(8,128)S(1)}, f32[512,384]{1,0:T(8,128)}, u32[]{:S(2)}) copy-start(f32[512,384]{1,0:T(8,128)} %coupling_hbm.1) | copy-start | bytes 2359300
  4.9 1.1 %copy-start.3 = (f32[384,384]{1,0:T(8,128)S(1)}, f32[384,384]{1,0:T(8,128)}, u32[]{:S(2)}) copy-start(f32[384,384]{1,0:T(8,128)} %operator_hbm.1) | copy-start | bytes 1769476

commit v2 on v1

--- a/solution.py
+++ b/solution.py
@@ -648,13 +648,18 @@
                 collective_id=0, has_side_effects=True, vmem_limit_bytes=32 << 20
             ),
         )(
-            flat,
-            inverse,
-            coupling,
-            operator,
-            face_ids.T,
-            orientation.T,
-            scale.reshape(1, ELEMENTS),
+            *(
+                pltpu.with_memory_space_constraint(value, pltpu.HBM)
+                for value in (
+                    flat,
+                    inverse,
+                    coupling,
+                    operator,
+                    face_ids.T,
+                    orientation.T,
+                    scale.reshape(1, ELEMENTS),
+                )
+            )
         )
         interior, sides, tops = pl.pallas_call(
             combine,

time: 60 us -> 55.9 us (0.932)
  local copies, waits for them, and re-layouts: 5.32 us -> 0 us
  Pallas kernels: 53.8 us -> 55.2 us
    unnamed x14 -> x0, local copies, waits for them, and re-layouts: 5.32 us -> none
    pallas_call x1, Pallas kernels: 52.4 us -> 53.9 us  [per_device(): pl.pallas_call(functools.partial(kernel, layers, blocks), out_shape=tuple...]
where the time goes in v2:
time: 55.9 us
  Pallas kernels  55.2 us (99%)
  between operations  0.64 us (1%)
    pallas_call x1, Pallas kernels, per_device(): pl.pallas_call(functools.partial(kernel, layers, blocks), out_shape=tuple...  53.9 us
    pallas_call x1, Pallas kernels, per_device(): pl.pallas_call(combine, out_shape=(shapes[0], shapes[3], shapes[5]), in_s...  1.35 us

profile of v2, /device:TPU:1, one launch (start us, length us, event | category | flops | bytes accessed | tf_op | source)
XLA Modules:
  0.0 55.9 jit_solution(18317932895762843564)
XLA Ops:
  0.6 53.9 %shard_map.94 = (f32[512,512]{1,0:T(8,128)S(1)}, f32[512,512]{1,0:T(8,128)S(1)}, f32[512,512]{1,0:T(8,128)S(1)}, f32[512,128]{1,0:T(8,128)S(1)}, f32[512,128]{1,...) custom-call(f32[512,512]{1,0:T(8,128)} %bitcast.11, f32[512,512]{1,0:T(8,128)} %inverse_hbm.1, ...), custom_call_target="tpu_custom_call" | custom-call | tf_op jit(solution)/shard_map/pallas_call | solution.py:606
  54.5 1.3 %shard_map.95 = (f32[512,512]{1,0:T(8,128)}, f32[512,128]{1,0:T(8,128)}, f32[512,64]{1,0:T(8,128)}) custom-call(f32[16,128]{1,0:T(8,128)S(1)} %get-tuple-element.14.weights, f32[512,512]{1,0:T(8,128)S(1)} %get-tuple-element.15.solved, f32[512,512]{1,0:T(8,128)S(1)} %get-tuple-element.16.moved_zero, f32[512,512]{1,0:T(8,128)S(1)} %get-tuple-element.17.moved_one, ...), custom_call_target="tpu_custom_call" | custom-call | tf_op jit(solution)/shard_map/pallas_call | solution.py:664

commit v3 on v2

--- a/solution.py
+++ b/solution.py
@@ -19,16 +19,22 @@
 PAIRS = RIGHT // 2
 
 
-def partner(me, turn, count):
-    if count != 64:
-        return (me + 1 + turn) % count
-    far_z, far_y, far_core = turn // 8, turn % 8 // 2, turn % 2
-    step_z = (4 + (far_z + 1) // 2 * (1 - 2 * (far_z % 2))) % 8
-    step_y = (2 + (far_y + 1) // 2 * (1 - 2 * (far_y % 2))) % 4
-    z = (me // 8 + step_z) % 8
-    y = (me % 8 // 2 + step_y) % 4
-    core = (me % 2 + 1 - far_core) % 2
-    return z * 8 + y * 2 + core
+def turns(layers, blocks):
+    def ring(step, count):
+        return min(step, count - step)
+
+    deep = blocks // 8
+    steps = [
+        (x, z, y, core)
+        for x in range(layers)
+        for z in range(deep)
+        for y in range(4)
+        for core in (1, 0)
+        if (x, z, y, core) != (0, 0, 0, 0)
+    ]
+    return sorted(
+        steps, key=lambda step: (-ring(step[0], layers) - ring(step[1], deep) - ring(step[2], 4), step[3])
+    )
 
 
 def halves(value):
@@ -139,25 +145,26 @@
     me = lax.axis_index("dev")
     others = blocks - 1
     core = me % 2
-    core_pair = me // 2 * 2
+
+    deep = blocks // 8
+    along_x = [(layer + step) % layers for step in range(layers)]
+    along_z = [(me // 8 + step) % deep * 8 for step in range(deep)]
+    along_y = [(me % 8 // 2 + step) % 4 * 2 for step in range(4)]
+    along_core = [core, 1 - core]
+    everyone = [
+        (x, z, y, c, along_x[x], along_z[z] + along_y[y] + along_core[c])
+        for x, z, y, c in turns(layers, blocks)
+    ]
+    peers = [peer for x, *_, peer in everyone if x == 0]
+    column_peers = [(at, peer) for x, z, y, _, at, peer in everyone if z == 0 and y == 0]
+    far_peers = [peer for x, _, _, c, _, peer in everyone if x == 0 and c == 0]
 
     barrier = pltpu.get_barrier_semaphore()
-
-    def greet(turn, carry):
-        pl.semaphore_signal(
-            barrier, inc=1, device_id={"dev": partner(me, turn, blocks)}, device_id_type=MESH
-        )
-        return carry
-
-    lax.fori_loop(0, others, greet, 0)
-    for step in range(1, layers):
-        for side in range(2):
-            pl.semaphore_signal(
-                barrier,
-                inc=1,
-                device_id=((layer + step) % layers, core_pair + (core + side) % 2),
-                device_id_type=MESH,
-            )
+    for peer in peers:
+        pl.semaphore_signal(barrier, inc=1, device_id=(layer, peer), device_id_type=MESH)
+    for at, peer in column_peers:
+        if at is not along_x[0]:
+            pl.semaphore_signal(barrier, inc=1, device_id=(at, peer), device_id_type=MESH)
 
     loads = [
         pltpu.make_async_copy(inverse_hbm, inverse, load_sem.at[0]),
@@ -172,7 +179,7 @@
         load.start()
 
     here = pl.ds(pl.multiple_of(me * 8, 8), 8)
-    for phase in range(3):
+    for phase in range(4):
         received[phase, here, :] = jnp.zeros((8, LANES), F32)
 
     @pl.when(layer == 0)
@@ -208,15 +215,15 @@
     near = onehot(first_col + me * LANES == second_row).astype(BF16)
     near_back = onehot(first_row + me * LANES == second_col).astype(BF16)
     into_faces = onehot(first_row == row_of(square)).astype(BF16)
-    peers = (blocks, LANES)
+    peer_shape = (blocks, LANES)
     owner_row = second_row[:blocks] // LANES
-    peer_row = row_of(peers)
+    peer_row = row_of(peer_shape)
     to_owner_f = onehot((owner_row == peer_row) & (peer_row != me))
     to_owner = to_owner_f.astype(BF16)
     from_owner = jnp.transpose(to_owner_f).astype(BF16)
     slot_number = (second_row[:blocks] % LANES + 1).astype(F32)
     named = jnp.sum(to_owner_f * slot_number, axis=1, keepdims=True)
-    sent[0, pl.ds(4, blocks, stride=8), :] = jnp.broadcast_to(named, peers)
+    sent[3, pl.ds(0, blocks, stride=8), :] = jnp.broadcast_to(named, peer_shape)
 
     lane = lane_of((ELEMENTS, LANES))
     low = lane < 64
@@ -319,19 +326,15 @@
             up_copy(phase).wait_recv()
 
     def send_rows(phase, rows):
-        def send(turn, carry):
-            peer = partner(me, turn, blocks)
+        for peer in peers:
             pltpu.make_async_remote_copy(
                 sent.at[phase, pl.ds(pl.multiple_of(peer * 8, 8), rows)],
                 received.at[phase, pl.ds(pl.multiple_of(me * 8, 8), rows)],
                 swap_sem.at[phase, 0],
                 swap_sem.at[phase, 1],
-                device_id={"dev": peer},
+                device_id=(layer, peer),
                 device_id_type=MESH,
             ).start()
-            return carry
-
-        lax.fori_loop(0, others, send, 0)
 
     def wait_sent(phase, rows):
         wait_rows(sent.at[phase], others * rows, swap_sem.at[phase, 0])
@@ -361,63 +364,55 @@
         ref[spot] = value
         vector_h[spot], vector_l[spot] = halves(value)
 
-    def sum_peer(turn):
-        step = (layers // 2 + (turn // 2 + 1) // 2 * (1 - 2 * (turn // 2 % 2))) % layers
-        return (layer + step) % layers, core_pair + (core + 1 - turn % 2) % 2
-
-    def far_peer(turn):
-        if blocks == 64:
-            return partner(me, 2 * turn + 1, blocks)
-        return (me + 2 * (turn + 1)) % blocks
-
-    def start_sum(phase, quantities):
+    def summed(quantities):
         lanes = lane_of((RIGHT, LANES))
         place = row_of((RIGHT, LANES))
         spread = jnp.zeros((RIGHT, LANES), F32)
         for number, rows in enumerate(quantities):
             total = jnp.sum(jnp.concatenate(rows, axis=0), axis=1, keepdims=True)
             spread = jnp.where(lanes == place + number * RIGHT, total, spread)
-        mine = jnp.sum(spread, axis=0, keepdims=True)
-        near_out[phase] = mine
-        near_in[phase, layer * 2 + core] = mine
-
-        def send(turn, carry):
+        return jnp.sum(spread, axis=0, keepdims=True)
+
+    def share(mine, out_ref, in_ref, place, sem, targets):
+        out_ref[...] = mine
+        in_ref[place] = mine
+        for at, peer in targets:
             pltpu.make_async_remote_copy(
-                near_out.at[phase],
-                near_in.at[phase, layer * 2 + core],
-                near_sem.at[phase, 0],
-                near_sem.at[phase, 1],
-                device_id=sum_peer(turn),
+                out_ref,
+                in_ref.at[place],
+                sem.at[0],
+                sem.at[1],
+                device_id=(at, peer),
                 device_id_type=MESH,
             ).start()
-            return carry
-
-        lax.fori_loop(0, 2 * layers - 1, send, 0)
-
-    def middle_sum(phase):
-        wait_rows(near_in.at[phase], 2 * layers - 1, near_sem.at[phase, 1])
-        wait_rows(near_in.at[phase], 2 * layers - 1, near_sem.at[phase, 0])
-        mine = jnp.sum(near_in[phase], axis=0)
-        far_out[phase] = mine
-        far_in[phase, me // 2] = mine
-
-        def send(turn, carry):
-            pltpu.make_async_remote_copy(
-                far_out.at[phase],
-                far_in.at[phase, me // 2],
-                far_sem.at[phase, 0],
-                far_sem.at[phase, 1],
-                device_id={"dev": far_peer(turn)},
-                device_id_type=MESH,
-            ).start()
-            return carry
-
-        lax.fori_loop(0, blocks // 2 - 1, send, 0)
-
-    def finish_sum(phase, count):
-        wait_rows(far_in.at[phase], blocks // 2 - 1, far_sem.at[phase, 1])
-        wait_rows(far_in.at[phase], blocks // 2 - 1, far_sem.at[phase, 0])
-        total = jnp.broadcast_to(jnp.sum(far_in[phase], axis=0), (RIGHT, LANES))
+
+    def shared(in_ref, sem, count):
+        wait_rows(in_ref, count, sem.at[1])
+        wait_rows(in_ref, count, sem.at[0])
+        return jnp.sum(in_ref[...], axis=0)
+
+    def share_near(phase, quantities):
+        share(
+            summed(quantities),
+            near_out.at[phase],
+            near_in.at[phase],
+            layer * 2 + core,
+            near_sem.at[phase],
+            column_peers,
+        )
+
+    def share_far(phase):
+        share(
+            shared(near_in.at[phase], near_sem.at[phase], len(column_peers)),
+            far_out.at[phase],
+            far_in.at[phase],
+            me // 2,
+            far_sem.at[phase],
+            [(layer, peer) for peer in far_peers],
+        )
+
+    def columns_of(row, count):
+        total = jnp.broadcast_to(row, (RIGHT, LANES))
         lanes = lane_of((RIGHT, LANES))
         place = row_of((RIGHT, LANES))
         return [
@@ -429,6 +424,9 @@
             )
             for number in range(count)
         ]
+
+    def finish_far(phase, count):
+        return columns_of(shared(far_in.at[phase], far_sem.at[phase], len(far_peers)), count)
 
     def owned_square(values):
         kept = values[0] * values[0] + jnp.where(low, 0.0, values[2] * values[2])
@@ -475,19 +473,21 @@
     put(0, 0, pick(to_owner, slots_second[...]))
     pl.semaphore_wait(barrier, others + 2 * (layers - 1))
 
-    send_rows(0, 5)
+    send_rows(3, 1)
+    send_rows(0, 4)
     start_ends(0)
     solved[...] = dot_three(source_h[...], source_l[...], inverse_h[...], inverse_l[...])
     loads[3].wait()
     operator_h[...], operator_l[...] = halves(operator[...])
     nearby_first = pick(near, slots_second[...])
-    wait_received(0, 5)
-    to_holder_f = onehot(got(0, 4).astype(jnp.int32) == first_row[:blocks] + 1)
+    wait_received(3, 1)
+    to_holder_f = onehot(got(3, 0).astype(jnp.int32) == first_row[:blocks] + 1)
     to_holder = to_holder_f.astype(BF16)
     from_holder = jnp.transpose(to_holder_f).astype(BF16)
 
     put(1, 0, pick(to_holder, slots_first[...]))
     send_rows(1, 4)
+    wait_received(0, 4)
     for pair in range(PAIRS):
         value = nearby_first[:, lanes_of(pair)] + pick(from_holder, got(0, pair))
         for right, part in arrivals(0, pair, value):
@@ -513,8 +513,9 @@
         mine = chunks_of(first, right)
         squares.append(owned_square(mine))
         curves.append(inner_rows(mine, chunks_of(image, right)))
-    start_sum(0, [squares, curves])
-    wait_sent(0, 5)
+    share_near(0, [squares, curves])
+    wait_sent(3, 1)
+    wait_sent(0, 4)
     wait_sent(1, 4)
     to_slots(image, (1, 0, 2), stores)
     put(2, 0, pick(to_owner, slots_second[...]))
@@ -522,7 +523,7 @@
     send_rows(2, 8)
     start_ends(1)
 
-    middle_sum(0)
+    share_far(0)
     nearby_first = pick(near, slots_second[...])
     nearby_second = pick(near_back, slots_first[...])
     for right in range(RIGHT):
@@ -548,7 +549,7 @@
                 keep(update, spot, image[spot] + part)
     second_image[...] = operated((0, 1, 2))
 
-    norm, curve = finish_sum(0, 2)
+    norm, curve = finish_far(0, 2)
     alpha = norm / curve
     squares, crosses, curves = [], [], []
     for right in range(RIGHT):
@@ -560,12 +561,12 @@
         squares.append(owned_square(mine))
         crosses.append(inner_rows(mine, old))
         curves.append(inner_rows(mine, new))
-    start_sum(1, [squares, crosses, curves])
+    share_near(1, [squares, crosses, curves])
 
     moved_one[...] = dot_three(vector_h[...], vector_l[...], merged_th[...], merged_tl[...])
-    middle_sum(1)
+    share_far(1)
     face_values(update, sides_one, tops_one)
-    norm_next, cross, curve_next = finish_sum(1, 3)
+    norm_next, cross, curve_next = finish_far(1, 3)
     beta = norm_next / norm
     curve_next = curve_next + 2.0 * beta * cross + beta * beta * curve
     weight_update = norm_next / curve_next
@@ -631,14 +632,14 @@
                 *[vmem((128, 512), F32)] * 2,
                 *[vmem((256, 128), F32)] * 2,
                 vmem((ROWS, LOCAL), F32),
-                *[vmem((3, blocks * 8, LANES), F32)] * 2,
+                *[vmem((4, blocks * 8, LANES), F32)] * 2,
                 *[vmem((2, 256, 128), F32)] * 2,
                 vmem((2, 1, LANES), F32),
                 vmem((2, 2 * layers, 1, LANES), F32),
                 vmem((2, 1, LANES), F32),
                 vmem((2, blocks // 2, 1, LANES), F32),
                 dma((7,)),
-                dma((3, 2)),
+                dma((4, 2)),
                 dma((2, 2)),
                 dma((2, 2)),
                 dma((2, 2)),

time: 55.9 us -> 48.8 us (0.87)
  Pallas kernels: 55.2 us -> 48.1 us
    pallas_call x1, Pallas kernels: 53.9 us -> 46.7 us  [per_device(): pl.pallas_call(functools.partial(kernel, layers, blocks), out_shape=tuple...]
where the time goes in v3:
time: 48.8 us; the launch traced here: 48.7 us
  Pallas kernels  48.1 us (99%)
  between operations  0.64 us (1%)
    pallas_call x1, Pallas kernels, per_device(): pl.pallas_call(functools.partial(kernel, layers, blocks), out_shape=tuple...  46.7 us
    pallas_call x1, Pallas kernels, per_device(): pl.pallas_call(combine, out_shape=(shapes[0], shapes[3], shapes[5]), in_s...  1.35 us

profile of v3, /device:TPU:1, one launch (start us, length us, event | category | flops | bytes accessed | tf_op | source)
XLA Modules:
  0.0 48.7 jit_solution(15038804083409951755)
XLA Ops:
  0.6 46.7 %shard_map.94 = (f32[512,512]{1,0:T(8,128)S(1)}, f32[512,512]{1,0:T(8,128)S(1)}, f32[512,512]{1,0:T(8,128)S(1)}, f32[512,128]{1,0:T(8,128)S(1)}, f32[512,128]{1,...) custom-call(f32[512,512]{1,0:T(8,128)} %bitcast.11, f32[512,512]{1,0:T(8,128)} %inverse_hbm.1, ...), custom_call_target="tpu_custom_call" | custom-call | tf_op jit(solution)/shard_map/pallas_call | solution.py:607
  47.4 1.3 %shard_map.95 = (f32[512,512]{1,0:T(8,128)}, f32[512,128]{1,0:T(8,128)}, f32[512,64]{1,0:T(8,128)}) custom-call(f32[16,128]{1,0:T(8,128)S(1)} %get-tuple-element.14.weights, f32[512,512]{1,0:T(8,128)S(1)} %get-tuple-element.15.solved, f32[512,512]{1,0:T(8,128)S(1)} %get-tuple-element.16.moved_zero, f32[512,512]{1,0:T(8,128)S(1)} %get-tuple-element.17.moved_one, ...), custom_call_target="tpu_custom_call" | custom-call | tf_op jit(solution)/shard_map/pallas_call | solution.py:665

commit v4 on v3

--- a/solution.py
+++ b/solution.py
@@ -50,9 +50,12 @@
     return dot(left_high, right_high) + (dot(left_high, right_low) + dot(left_low, right_high))
 
 
-def pick(onehot, value):
-    high, low = halves(value)
-    return dot(onehot, high) + dot(onehot, low)
+def twice(onehot):
+    return jnp.concatenate([onehot, onehot], axis=1)
+
+
+def pick(onehots, value):
+    return dot(onehots, jnp.concatenate(halves(value), axis=0))
 
 
 def lane_of(shape):
@@ -106,11 +109,11 @@
     inverse_l,
     coupling_h,
     coupling_l,
-    operator_h,
+    operator_hh,
     operator_l,
     merged_h,
     merged_l,
-    merged_th,
+    merged_thh,
     merged_tl,
     table,
     index_to,
@@ -119,8 +122,7 @@
     first,
     image,
     update,
-    vector_h,
-    vector_l,
+    vector,
     slots_first,
     slots_second,
     bottoms,
@@ -179,7 +181,7 @@
         load.start()
 
     here = pl.ds(pl.multiple_of(me * 8, 8), 8)
-    for phase in range(4):
+    for phase in range(5):
         received[phase, here, :] = jnp.zeros((8, LANES), F32)
 
     @pl.when(layer == 0)
@@ -212,15 +214,15 @@
     def onehot(condition):
         return jnp.where(condition, 1.0, 0.0).astype(F32)
 
-    near = onehot(first_col + me * LANES == second_row).astype(BF16)
-    near_back = onehot(first_row + me * LANES == second_col).astype(BF16)
-    into_faces = onehot(first_row == row_of(square)).astype(BF16)
+    near = twice(onehot(first_col + me * LANES == second_row).astype(BF16))
+    near_back = twice(onehot(first_row + me * LANES == second_col).astype(BF16))
+    into_faces = twice(onehot(first_row == row_of(square)).astype(BF16))
     peer_shape = (blocks, LANES)
     owner_row = second_row[:blocks] // LANES
     peer_row = row_of(peer_shape)
     to_owner_f = onehot((owner_row == peer_row) & (peer_row != me))
-    to_owner = to_owner_f.astype(BF16)
-    from_owner = jnp.transpose(to_owner_f).astype(BF16)
+    to_owner = twice(to_owner_f.astype(BF16))
+    from_owner = twice(jnp.transpose(to_owner_f).astype(BF16))
     slot_number = (second_row[:blocks] % LANES + 1).astype(F32)
     named = jnp.sum(to_owner_f * slot_number, axis=1, keepdims=True)
     sent[3, pl.ds(0, blocks, stride=8), :] = jnp.broadcast_to(named, peer_shape)
@@ -361,8 +363,11 @@
                 yield spot, jnp.where(live, image[spot] + part, 0.0)
 
     def keep(ref, spot, value):
+        rows, lanes = spot
         ref[spot] = value
-        vector_h[spot], vector_l[spot] = halves(value)
+        high, low_part = halves(value)
+        vector[rows, 2 * lanes.start : 2 * lanes.start + LANES] = high
+        vector[rows, 2 * lanes.start + LANES : 2 * lanes.stop] = low_part
 
     def summed(quantities):
         lanes = lane_of((RIGHT, LANES))
@@ -439,16 +444,23 @@
     def chunks_of(ref, right):
         return [ref[rows_of(right), lanes_of(chunk)] for chunk in range(3)]
 
-    def operated(chunks):
+    def stacked(chunk):
+        return slice(2 * chunk * LANES, 2 * (chunk + 1) * LANES)
+
+    def applied(double_ref, low_ref, chunks):
         return sum(
-            dot_three(
-                vector_h[:, lanes_of(chunk)],
-                vector_l[:, lanes_of(chunk)],
-                operator_h[lanes_of(chunk), :],
-                operator_l[lanes_of(chunk), :],
+            dot(vector[:, stacked(chunk)], double_ref[stacked(chunk), :])
+            + dot(
+                vector[:, 2 * chunk * LANES : (2 * chunk + 1) * LANES], low_ref[lanes_of(chunk), :]
             )
             for chunk in chunks
         )
+
+    def hold(double_ref, low_ref, value):
+        high, low_part = halves(value)
+        low_ref[...] = low_part
+        for chunk in range(3):
+            double_ref[stacked(chunk), :] = jnp.concatenate([high[lanes_of(chunk)]] * 2, axis=0)
 
     def face_values(vector, sides_ref, tops_ref):
         for pair in range(PAIRS):
@@ -478,12 +490,16 @@
     start_ends(0)
     solved[...] = dot_three(source_h[...], source_l[...], inverse_h[...], inverse_l[...])
     loads[3].wait()
-    operator_h[...], operator_l[...] = halves(operator[...])
+    hold(operator_hh, operator_l, operator[...])
+    for right in range(RIGHT):
+        for part in range(4):
+            solved[rows_of(right), lanes_of(part)] = solved[rows_of(right), lanes_of(part)] / scales[...]
+    hold(merged_thh, merged_tl, jnp.transpose(merged_h[...].astype(F32) + merged_l[...].astype(F32)))
     nearby_first = pick(near, slots_second[...])
     wait_received(3, 1)
     to_holder_f = onehot(got(3, 0).astype(jnp.int32) == first_row[:blocks] + 1)
-    to_holder = to_holder_f.astype(BF16)
-    from_holder = jnp.transpose(to_holder_f).astype(BF16)
+    to_holder = twice(to_holder_f.astype(BF16))
+    from_holder = twice(jnp.transpose(to_holder_f).astype(BF16))
 
     put(1, 0, pick(to_holder, slots_first[...]))
     send_rows(1, 4)
@@ -496,7 +512,7 @@
     finish_ends(0)
     for spot, value in end_arrivals(0):
         keep(first, spot, value)
-    second_image[...] = operated((0, 2))
+    second_image[...] = applied(operator_hh, operator_l, (0, 2))
     nearby_second = pick(near_back, slots_first[...])
     wait_received(1, 4)
     for pair in range(PAIRS):
@@ -504,7 +520,7 @@
         for right, part in arrivals(1, pair, value):
             spot = rows_of(right), lanes_of(1)
             keep(first, spot, image[spot] + part)
-    image[...] = second_image[...] + operated((1,))
+    image[...] = second_image[...] + applied(operator_hh, operator_l, (1,))
 
     squares, curves = [], []
     for right in range(RIGHT):
@@ -519,35 +535,35 @@
     wait_sent(1, 4)
     to_slots(image, (1, 0, 2), stores)
     put(2, 0, pick(to_owner, slots_second[...]))
-    put(2, 4, pick(to_holder, slots_first[...]))
-    send_rows(2, 8)
+    send_rows(2, 4)
+    put(4, 0, pick(to_holder, slots_first[...]))
+    send_rows(4, 4)
     start_ends(1)
 
-    share_far(0)
     nearby_first = pick(near, slots_second[...])
     nearby_second = pick(near_back, slots_first[...])
-    for right in range(RIGHT):
-        for part in range(4):
-            solved[rows_of(right), lanes_of(part)] = solved[rows_of(right), lanes_of(part)] / scales[...]
-    merged_th[...] = jnp.transpose(merged_h[...].astype(F32)).astype(BF16)
-    merged_tl[...] = jnp.transpose(merged_l[...].astype(F32)).astype(BF16)
-    moved_zero[...] = dot_three(vector_h[...], vector_l[...], merged_th[...], merged_tl[...])
+    moved_zero[...] = applied(merged_thh, merged_tl, (0, 1, 2))
     face_values(first, sides_zero, tops_zero)
+    share_far(0)
     finish_ends(1)
     for spot, value in end_arrivals(1):
         keep(update, spot, value)
-    wait_received(2, 8)
-    wait_sent(2, 8)
+    wait_received(2, 4)
     for pair in range(PAIRS):
-        arrived = (
-            nearby_first[:, lanes_of(pair)] + pick(from_holder, got(2, pair)),
-            nearby_second[:, lanes_of(pair)] + pick(from_owner, got(2, pair + 4)),
-        )
-        for chunk in range(2):
-            for right, part in arrivals(chunk, pair, arrived[chunk]):
-                spot = rows_of(right), lanes_of(chunk)
-                keep(update, spot, image[spot] + part)
-    second_image[...] = operated((0, 1, 2))
+        value = nearby_first[:, lanes_of(pair)] + pick(from_holder, got(2, pair))
+        for right, part in arrivals(0, pair, value):
+            spot = rows_of(right), lanes_of(0)
+            keep(update, spot, image[spot] + part)
+    second_image[...] = applied(operator_hh, operator_l, (0, 2))
+    wait_received(4, 4)
+    for pair in range(PAIRS):
+        value = nearby_second[:, lanes_of(pair)] + pick(from_owner, got(4, pair))
+        for right, part in arrivals(1, pair, value):
+            spot = rows_of(right), lanes_of(1)
+            keep(update, spot, image[spot] + part)
+    second_image[...] = second_image[...] + applied(operator_hh, operator_l, (1,))
+    wait_sent(2, 4)
+    wait_sent(4, 4)
 
     norm, curve = finish_far(0, 2)
     alpha = norm / curve
@@ -563,7 +579,7 @@
         curves.append(inner_rows(mine, new))
     share_near(1, [squares, crosses, curves])
 
-    moved_one[...] = dot_three(vector_h[...], vector_l[...], merged_th[...], merged_tl[...])
+    moved_one[...] = applied(merged_thh, merged_tl, (0, 1, 2))
     share_far(1)
     face_values(update, sides_one, tops_one)
     norm_next, cross, curve_next = finish_far(1, 3)
@@ -574,19 +590,48 @@
     weights[8:16, :] = weight_update * alpha
 
 
-def combine(weights, solved, moved_zero, moved_one, sides_zero, sides_one, tops_zero, tops_one, interior, sides, tops):
+def combine(
+    weights,
+    solved,
+    moved_zero,
+    moved_one,
+    sides_zero,
+    sides_one,
+    tops_zero,
+    tops_one,
+    interior_hbm,
+    sides_hbm,
+    tops_hbm,
+    interior,
+    sides,
+    tops,
+    sem,
+):
+    writes = []
+
+    def write(here, there, rows):
+        writes.append(pltpu.make_async_copy(here.at[rows], there.at[rows], sem.at[len(writes)]))
+        writes[-1].start()
+
     for right in range(RIGHT):
+        rows = slice(right * 64, right * 64 + 64)
         for part in range(4):
-            spot = slice(right * 64, right * 64 + 64), slice(part * LANES, part * LANES + LANES)
+            spot = rows, slice(part * LANES, part * LANES + LANES)
             interior[spot] = (
                 solved[spot]
                 - weights[right : right + 1, :] * moved_zero[spot]
                 + weights[8 + right : 9 + right, :] * moved_one[spot]
             )
+        if right % 2 == 1:
+            write(interior, interior_hbm, pl.ds(right * 64 - 64, 128))
     for node in range(64):
         spot = slice(node * 8, node * 8 + 8)
         sides[spot, :] = weights[0:8, :] * sides_zero[spot, :] - weights[8:16, :] * sides_one[spot, :]
         tops[spot, :] = weights[0:8, :64] * tops_zero[spot, :] - weights[8:16, :64] * tops_one[spot, :]
+    write(sides, sides_hbm, pl.ds(0, 512))
+    write(tops, tops_hbm, pl.ds(0, 512))
+    for started in writes:
+        started.wait()
 
 
 def solution(mesh):
@@ -620,26 +665,28 @@
                 *[vmem((ROWS, NODES), BF16)] * 2,
                 *[vmem((NODES, NODES), BF16)] * 2,
                 *[vmem((NODES, LOCAL), BF16)] * 2,
-                *[vmem((LOCAL, LOCAL), BF16)] * 2,
+                vmem((2 * LOCAL, LOCAL), BF16),
+                vmem((LOCAL, LOCAL), BF16),
                 *[vmem((NODES, LOCAL), BF16)] * 2,
-                *[vmem((LOCAL, NODES), BF16)] * 2,
+                vmem((2 * LOCAL, NODES), BF16),
+                vmem((LOCAL, NODES), BF16),
                 vmem((LANES, LANES), F32),
                 vmem((3, ELEMENTS, LANES), jnp.int32),
                 vmem((3, ELEMENTS, LANES), jnp.int32),
                 vmem((ELEMENTS, LANES), F32),
                 *[vmem((ROWS, LOCAL), F32)] * 3,
-                *[vmem((ROWS, LOCAL), BF16)] * 2,
+                vmem((ROWS, 2 * LOCAL), BF16),
                 *[vmem((128, 512), F32)] * 2,
                 *[vmem((256, 128), F32)] * 2,
                 vmem((ROWS, LOCAL), F32),
-                *[vmem((4, blocks * 8, LANES), F32)] * 2,
+                *[vmem((5, blocks * 8, LANES), F32)] * 2,
                 *[vmem((2, 256, 128), F32)] * 2,
                 vmem((2, 1, LANES), F32),
                 vmem((2, 2 * layers, 1, LANES), F32),
                 vmem((2, 1, LANES), F32),
                 vmem((2, blocks // 2, 1, LANES), F32),
                 dma((7,)),
-                dma((4, 2)),
+                dma((5, 2)),
                 dma((2, 2)),
                 dma((2, 2)),
                 dma((2, 2)),
@@ -666,7 +713,13 @@
             combine,
             out_shape=(shapes[0], shapes[3], shapes[5]),
             in_specs=[local] * 8,
-            out_specs=(local,) * 3,
+            out_specs=(pl.BlockSpec(memory_space=pl.ANY),) * 3,
+            scratch_shapes=[
+                vmem((ROWS, NODES), F32),
+                vmem((512, 128), F32),
+                vmem((512, 64), F32),
+                dma((6,)),
+            ],
             compiler_params=pltpu.CompilerParams(vmem_limit_bytes=16 << 20),
         )(weights, *found)
         return (

time: 48.8 us -> 47.9 us (0.982)
  Pallas kernels: 48.1 us -> 47.2 us
    pallas_call x1, Pallas kernels: 46.7 us -> 45.9 us  [per_device(): pl.pallas_call(functools.partial(kernel, layers, blocks), out_shape=tuple...]
where the time goes in v4:
time: 47.9 us; the launch traced here: 47.8 us
  Pallas kernels  47.2 us (99%)
  between operations  0.64 us (1%)
    pallas_call x1, Pallas kernels, per_device(): pl.pallas_call(functools.partial(kernel, layers, blocks), out_shape=tuple...  45.9 us
    pallas_call x1, Pallas kernels, per_device(): pl.pallas_call(combine, out_shape=(shapes[0], shapes[3], shapes[5]), in_s...  1.24 us

profile of v4, /device:TPU:1, one launch (start us, length us, event | category | flops | bytes accessed | tf_op | source)
XLA Modules:
  0.0 47.8 jit_solution(17877363143030145436)
XLA Ops:
  0.6 45.9 %shard_map.94 = (f32[512,512]{1,0:T(8,128)S(1)}, f32[512,512]{1,0:T(8,128)S(1)}, f32[512,512]{1,0:T(8,128)S(1)}, f32[512,128]{1,0:T(8,128)S(1)}, f32[512,128]{1,...) custom-call(f32[512,512]{1,0:T(8,128)} %bitcast.11, f32[512,512]{1,0:T(8,128)} %inverse_hbm.1, ...), custom_call_target="tpu_custom_call" | custom-call | tf_op jit(solution)/shard_map/pallas_call | solution.py:652
  46.6 1.2 %shard_map.95 = (f32[512,512]{1,0:T(8,128)}, f32[512,128]{1,0:T(8,128)}, f32[512,64]{1,0:T(8,128)}) custom-call(f32[16,128]{1,0:T(8,128)S(1)} %get-tuple-element.14.weights, f32[512,512]{1,0:T(8,128)S(1)} %get-tuple-element.15.solved, f32[512,512]{1,0:T(8,128)S(1)} %get-tuple-element.16.moved_zero, f32[512,512]{1,0:T(8,128)S(1)} %get-tuple-element.17.moved_one, ...), custom_call_target="tpu_custom_call" | custom-call | tf_op jit(solution)/shard_map/pallas_call | solution.py:712

commit v5 on v4

--- a/solution.py
+++ b/solution.py
@@ -136,12 +136,18 @@
     near_in,
     far_out,
     far_in,
+    pair_out,
+    pair_in,
+    all_out,
+    all_in,
     load_sem,
     swap_sem,
     up_sem,
     down_sem,
     near_sem,
     far_sem,
+    pair_sem,
+    all_sem,
 ):
     layer = lax.axis_index("gz")
     me = lax.axis_index("dev")
@@ -520,22 +526,33 @@
         for right, part in arrivals(1, pair, value):
             spot = rows_of(right), lanes_of(1)
             keep(first, spot, image[spot] + part)
-    image[...] = second_image[...] + applied(operator_hh, operator_l, (1,))
-
+
+    wait_sent(3, 1)
+    wait_sent(0, 4)
+    wait_sent(1, 4)
+
+    def finish_image(chunk):
+        lanes = lanes_of(chunk)
+        more = dot(vector[:, stacked(1)], operator_hh[stacked(1), lanes]) + dot(
+            vector[:, 256:384], operator_l[128:256, lanes]
+        )
+        for right in range(RIGHT):
+            spot = rows_of(right), lanes
+            image[spot] = (second_image[spot] + more[rows_of(right)]) * scales[...]
+
+    finish_image(1)
+    to_slots(image, (1,), stores)
+    put(2, 0, pick(to_owner, slots_second[...]))
+    send_rows(2, 4)
+    finish_image(0)
+    finish_image(2)
     squares, curves = [], []
     for right in range(RIGHT):
-        for chunk in range(3):
-            image[rows_of(right), lanes_of(chunk)] = image[rows_of(right), lanes_of(chunk)] * scales[...]
         mine = chunks_of(first, right)
         squares.append(owned_square(mine))
         curves.append(inner_rows(mine, chunks_of(image, right)))
     share_near(0, [squares, curves])
-    wait_sent(3, 1)
-    wait_sent(0, 4)
-    wait_sent(1, 4)
-    to_slots(image, (1, 0, 2), stores)
-    put(2, 0, pick(to_owner, slots_second[...]))
-    send_rows(2, 4)
+    to_slots(image, (0, 2), stores)
     put(4, 0, pick(to_holder, slots_first[...]))
     send_rows(4, 4)
     start_ends(1)
@@ -567,7 +584,7 @@
 
     norm, curve = finish_far(0, 2)
     alpha = norm / curve
-    squares, crosses, curves = [], [], []
+    squares, curves = [], []
     for right in range(RIGHT):
         step = alpha[right : right + 1, :]
         before, change = chunks_of(first, right), chunks_of(update, right)
@@ -575,16 +592,22 @@
         mine = [before[chunk] - step * change[chunk] for chunk in range(3)]
         new = [old[chunk] - step * (turned_change[chunk] * scales[...]) for chunk in range(3)]
         squares.append(owned_square(mine))
-        crosses.append(inner_rows(mine, old))
         curves.append(inner_rows(mine, new))
-    share_near(1, [squares, crosses, curves])
-
+    share(summed([squares, curves]), pair_out, pair_in, core, pair_sem, [(layer, me - core + 1 - core)])
+
+    share(
+        shared(pair_in, pair_sem, 1),
+        all_out,
+        all_in,
+        layer * (blocks // 2) + me // 2,
+        all_sem,
+        [(at, peer) for _, _, _, c, at, peer in everyone if c == 0],
+    )
     moved_one[...] = applied(merged_thh, merged_tl, (0, 1, 2))
-    share_far(1)
     face_values(update, sides_one, tops_one)
-    norm_next, cross, curve_next = finish_far(1, 3)
+    norm_next, curve_next = columns_of(shared(all_in, all_sem, layers * blocks // 2 - 1), 2)
     beta = norm_next / norm
-    curve_next = curve_next + 2.0 * beta * cross + beta * beta * curve
+    curve_next = curve_next - beta * norm_next / alpha
     weight_update = norm_next / curve_next
     weights[0:8, :] = alpha + weight_update * beta + weight_update
     weights[8:16, :] = weight_update * alpha
@@ -685,12 +708,18 @@
                 vmem((2, 2 * layers, 1, LANES), F32),
                 vmem((2, 1, LANES), F32),
                 vmem((2, blocks // 2, 1, LANES), F32),
+                vmem((1, LANES), F32),
+                vmem((2, 1, LANES), F32),
+                vmem((1, LANES), F32),
+                vmem((layers * blocks // 2, 1, LANES), F32),
                 dma((7,)),
                 dma((5, 2)),
                 dma((2, 2)),
                 dma((2, 2)),
                 dma((2, 2)),
                 dma((2, 2)),
+                dma((2,)),
+                dma((2,)),
             ],
             compiler_params=pltpu.CompilerParams(
                 collective_id=0, has_side_effects=True, vmem_limit_bytes=32 << 20

time: 47.9 us -> 46.5 us (0.971)
  Pallas kernels: 47.2 us -> 45.8 us
    pallas_call x1, Pallas kernels: 45.9 us -> 44.5 us  [per_device(): pl.pallas_call(functools.partial(kernel, layers, blocks), out_shape=tuple...]
where the time goes in v5:
time: 46.5 us; the launch traced here: 46.4 us
  Pallas kernels  45.8 us (98%)
  between operations  0.64 us (1%)
    pallas_call x1, Pallas kernels, per_device(): pl.pallas_call(functools.partial(kernel, layers, blocks), out_shape=tuple...  44.5 us
    pallas_call x1, Pallas kernels, per_device(): pl.pallas_call(combine, out_shape=(shapes[0], shapes[3], shapes[5]), in_s...  1.24 us

profile of v5, /device:TPU:1, one launch (start us, length us, event | category | flops | bytes accessed | tf_op | source)
XLA Modules:
  0.0 46.4 jit_solution(5560817330405766891)
XLA Ops:
  0.6 44.5 %shard_map.94 = (f32[512,512]{1,0:T(8,128)S(1)}, f32[512,512]{1,0:T(8,128)S(1)}, f32[512,512]{1,0:T(8,128)S(1)}, f32[512,128]{1,0:T(8,128)S(1)}, f32[512,128]{1,...) custom-call(f32[512,512]{1,0:T(8,128)} %bitcast.11, f32[512,512]{1,0:T(8,128)} %inverse_hbm.1, ...), custom_call_target="tpu_custom_call" | custom-call | tf_op jit(solution)/shard_map/pallas_call | solution.py:675
  45.2 1.2 %shard_map.95 = (f32[512,512]{1,0:T(8,128)}, f32[512,128]{1,0:T(8,128)}, f32[512,64]{1,0:T(8,128)}) custom-call(f32[16,128]{1,0:T(8,128)S(1)} %get-tuple-element.14.weights, f32[512,512]{1,0:T(8,128)S(1)} %get-tuple-element.15.solved, f32[512,512]{1,0:T(8,128)S(1)} %get-tuple-element.16.moved_zero, f32[512,512]{1,0:T(8,128)S(1)} %get-tuple-element.17.moved_one, ...), custom_call_target="tpu_custom_call" | custom-call | tf_op jit(solution)/shard_map/pallas_call | solution.py:741

commit v6 on v5

--- a/solution.py
+++ b/solution.py
@@ -487,11 +487,11 @@
                         offset * 64 : (offset + 1) * 64
                     ]
 
-    to_slots(image, (2, 1, 0), stores)
+    pl.semaphore_wait(barrier, others + 2 * (layers - 1))
+
+    send_rows(3, 1)
+    to_slots(image, (1, 0, 2), stores)
     put(0, 0, pick(to_owner, slots_second[...]))
-    pl.semaphore_wait(barrier, others + 2 * (layers - 1))
-
-    send_rows(3, 1)
     send_rows(0, 4)
     start_ends(0)
     solved[...] = dot_three(source_h[...], source_l[...], inverse_h[...], inverse_l[...])

time: 46.5 us -> 46 us (0.989)
  Pallas kernels: 45.8 us -> 45.3 us
    pallas_call x1, Pallas kernels: 44.5 us -> 44 us  [per_device(): pl.pallas_call(functools.partial(kernel, layers, blocks), out_shape=tuple...]
where the time goes in v6:
time: 46 us; the launch traced here: 45.9 us
  Pallas kernels  45.3 us (98%)
  between operations  0.64 us (1%)
    pallas_call x1, Pallas kernels, per_device(): pl.pallas_call(functools.partial(kernel, layers, blocks), out_shape=tuple...  44 us
    pallas_call x1, Pallas kernels, per_device(): pl.pallas_call(combine, out_shape=(shapes[0], shapes[3], shapes[5]), in_s...  1.24 us

profile of v6, /device:TPU:1, one launch (start us, length us, event | category | flops | bytes accessed | tf_op | source)
XLA Modules:
  0.0 45.9 jit_solution(8238974028523664860)
XLA Ops:
  0.6 44.0 %shard_map.94 = (f32[512,512]{1,0:T(8,128)S(1)}, f32[512,512]{1,0:T(8,128)S(1)}, f32[512,512]{1,0:T(8,128)S(1)}, f32[512,128]{1,0:T(8,128)S(1)}, f32[512,128]{1,...) custom-call(f32[512,512]{1,0:T(8,128)} %bitcast.11, f32[512,512]{1,0:T(8,128)} %inverse_hbm.1, ...), custom_call_target="tpu_custom_call" | custom-call | tf_op jit(solution)/shard_map/pallas_call | solution.py:675
  44.7 1.2 %shard_map.95 = (f32[512,512]{1,0:T(8,128)}, f32[512,128]{1,0:T(8,128)}, f32[512,64]{1,0:T(8,128)}) custom-call(f32[16,128]{1,0:T(8,128)S(1)} %get-tuple-element.14.weights, f32[512,512]{1,0:T(8,128)S(1)} %get-tuple-element.15.solved, f32[512,512]{1,0:T(8,128)S(1)} %get-tuple-element.16.moved_zero, f32[512,512]{1,0:T(8,128)S(1)} %get-tuple-element.17.moved_one, ...), custom_call_target="tpu_custom_call" | custom-call | tf_op jit(solution)/shard_map/pallas_call | solution.py:741
